TPU v7x, 32 devices: a whole 2x2x4 slice. The times are simulated.
32 devices in a mesh: sec: 4 (over y, x), pen: 4 (over z), rhs: 2 (over core).
Axes of the slice: x: 2, y: 2, z: 4, core: 2. Of those that a mesh axis runs over, the one named last changes fastest.
Arguments:
- source: float32 [2, 4, 4, 128, 512], P(None, 'rhs', 'sec', None, 'pen'), may hold values from -8 to 8
- medium: float32 [4, 128, 512], P('sec', None, 'pen'), may hold values from 0 to 0.5
- damping: float32 [4, 128, 512], P('sec', None, 'pen'), may hold values from 0.05 to 0.8
- inv_x: float32 [4, 1], P('sec'), as said below
- inv_y: float32 [1, 128, 128], replicated, as said below
- inv_z: float32 [2, 256, 256], replicated, as said below
Outputs:
- solution: float32 [2, 4, 4, 128, 512], P(None, 'rhs', 'sec', None, 'pen')
Inputs may be any that keep to these rules, and one draw needn't show every extreme that they name: Each entry of inv_x (one per section, since a section has 1 layer) is near 0.5: 0.5 plus a small random term. `inv_y`: each block is 0.5 times the identity plus dense off-diagonal terms. `inv_z`: each block is 0.5 times the identity plus dense off-diagonal terms.
All inputs are finite; a program needn't handle non-finite values.
Results may differ from a plain program's by a relative error of at most 0.0001.
Values sent between devices are 32-bit elements; how exact they have to be, the bound alone decides.
No kernel may reach another device: no remote copies, remote signals or barrier semaphores. Data moves between devices by JAX's collectives and lax.ppermute only.
A program may use at most 64 MiB of HBM per device.

v0:
```python
import functools

import jax
import jax.numpy as jnp
from jax import lax
from jax.experimental import pallas as pl
from jax.experimental.pallas import tpu as pltpu
from jax.sharding import PartitionSpec as P


ITERS = 3
ROWS = 16
SPARE = 2**22
PAD = 8
F32, BF16 = jnp.float32, jnp.bfloat16

CORNER, C, CENTRE = 0.03, 10.0 / 3.0, 1.0 / 3.0
UP, UP_REST = 0.01, 0.05


def halves(value):
    high = value.astype(BF16)
    return high, (value - high.astype(F32)).astype(BF16)


def split(value):
    high = lax.reduce_precision(value, exponent_bits=8, mantissa_bits=7)
    return high.astype(BF16), (value - high).astype(BF16)


def dot(a, b):
    return jnp.dot(a, b, preferred_element_type=F32)


def section_kernel(parted, place, *refs):
    refs = list(refs)
    pieces = [[[refs.pop(0) for _ in range(n)] for _ in range(2)] for n in parted]
    trace, y_left, z_high, z_low, out, res, step, diag, y_in, zh_in, zl_in = refs
    parts, quarters, height, lanes = 2, res.shape[0], diag.shape[2], res.shape[2]
    y_blocks, y_size = y_left.shape[0], y_left.shape[1] // 2
    per_block = z_high.shape[1] // lanes
    chunks = height // ROWS
    lane = lax.broadcasted_iota(jnp.int32, (ROWS, lanes), 1)
    first, last = lane == 0, lane == lanes - 1

    pads = jnp.zeros((PAD, lanes), F32)
    for buffer in range(2):
        for q in range(quarters):
            for c in range(parts):
                step[buffer, q, c, :PAD] = pads
                step[buffer, q, c, PAD + height :] = pads

    def neighbours(buffer, c, base, weight):
        tall = []
        for q in range(quarters):
            here = step[buffer, q, c, pl.ds(PAD + base, ROWS)]
            above = step[buffer, q, c, pl.ds(PAD + base - 1, ROWS)]
            below = step[buffer, q, c, pl.ds(PAD + base + 1, ROWS)]
            tall.append(weight * here + (above + below))
        up = [pltpu.roll(piece, 1, 1) for piece in tall]
        down = [pltpu.roll(piece, lanes - 1, 1) for piece in tall]
        near = []
        for q in range(quarters):
            left = jnp.where(first, up[q - 1] if q > 0 else 0.0, up[q])
            right = jnp.where(last, down[q + 1] if q + 1 < quarters else 0.0, down[q])
            near.append(weight * tall[q] + (left + right))
        return near

    def over_chunks(body):
        def chunk(i, carry):
            body(pl.multiple_of(i * ROWS, ROWS))
            return carry

        lax.fori_loop(0, chunks, chunk, 0, unroll=True)

    def at(arrays, d):
        size = arrays[0].shape[0]
        return arrays[d // size], d % size

    def load(source, diagonal, before, gain):
        for q in range(quarters):
            for c in range(parts):
                step[1, q, c, PAD : PAD + height] = before[q, c * height : (c + 1) * height]
        for d in range(quarters):
            q = place[d]
            array, k = at(source, d)
            res[q] = array[k, : parts * height] * (1.0 / CORNER)
            array, k = at(diagonal, d)
            diag[q, 0] = array[k, :height] * (1.0 / CORNER) + (1.3 + CENTRE) / CORNER
            diag[q, 1] = array[k, height : 2 * height] * (1.0 / CORNER)

        def body(base):
            for c in range(parts):
                rows = pl.ds(c * height + base, ROWS)
                near = neighbours(1, c, base, 3.0)
                for q in range(quarters):
                    here = step[1, q, c, pl.ds(PAD + base, ROWS)]
                    value = res[q, rows] + (UP / CORNER) * near[q] + (UP_REST / CORNER) * here
                    res[q, rows] = value
                    step[0, q, c, pl.ds(PAD + base, ROWS)] = gain * value

        over_chunks(body)

    def apply(source, add, then):
        def body(base):
            near = [neighbours(source, c, base, C) for c in range(parts)]
            for q in range(quarters):
                du = [step[source, q, c, pl.ds(PAD + base, ROWS)] for c in range(parts)]
                real, imag = (diag[q, c, pl.ds(base, ROWS)] for c in range(parts))
                turned = [real * du[0] - imag * du[1], real * du[1] + imag * du[0]]
                for c in range(parts):
                    rows = pl.ds(c * height + base, ROWS)
                    if add is not None:
                        out[q, rows] = add(q, c, base, rows, du[c])
                    value = res[q, rows] - turned[c] + near[c][q]
                    res[q, rows] = value
                    then(q, c, base, rows, value)

        over_chunks(body)

    def for_y(q, c, base, rows, value):
        high, low = halves(value)
        y_in[q, c, 0, pl.ds(base, ROWS)] = high
        y_in[q, c, 1, pl.ds(base, ROWS)] = low

    def for_z(q, c, base, rows, value):
        zh_in[q, rows], zl_in[q, rows] = halves(value)

    def solve_y():
        for b in range(y_blocks):
            rows = slice(b * y_size, (b + 1) * y_size)
            for c in range(parts):
                for q in range(0, quarters, per_block):
                    both = jnp.concatenate(
                        [
                            jnp.concatenate([y_in[q + k, c, h, rows] for h in range(2)], axis=0)
                            for k in range(per_block)
                        ],
                        axis=1,
                    )
                    done = dot(y_left[b], both)
                    done = done[:y_size] + done[y_size:]
                    for k in range(per_block):
                        step[1, q + k, c, PAD + b * y_size : PAD + (b + 1) * y_size] = done[
                            :, k * lanes : (k + 1) * lanes
                        ]

    def solve_z(add):
        for b in range(quarters // per_block):
            span = range(b * per_block, (b + 1) * per_block)
            high = jnp.concatenate([zh_in[q] for q in span], axis=1)
            low = jnp.concatenate([zl_in[q] for q in span], axis=1)
            done = dot(high, z_low[b]) + dot(low, z_high[b]) + dot(high, z_high[b])
            for k, q in enumerate(span):
                piece = done[:, k * lanes : (k + 1) * lanes]
                if add:
                    out[q] += piece
                else:
                    for c in range(parts):
                        step[1, q, c, PAD : PAD + height] = piece[
                            c * height : (c + 1) * height
                        ]

    for index, (source, diagonal) in enumerate(pieces):
        gain = CORNER * source[0][0, 2 * height, :][None, :]
        load(source, diagonal, trace if index == 0 else out, gain)
        for q in range(quarters):
            out[q] = jnp.zeros(out.shape[1:], F32)

        def for_x(q, c, base, rows, value):
            step[0, q, c, pl.ds(PAD + base, ROWS)] = gain * value

        def two_steps(q, c, base, rows, du):
            return out[q, rows] + (step[0, q, c, pl.ds(PAD + base, ROWS)] + du)

        def one_step(q, c, base, rows, du):
            return out[q, rows] + du

        def sweep(i, carry):
            apply(0, None, for_y)
            solve_y()
            apply(1, two_steps, for_z)

            @pl.when(i + 1 < ITERS)
            def _():
                solve_z(False)
                apply(1, one_step, for_x)

            return carry

        lax.fori_loop(0, ITERS, sweep, 0)
        solve_z(True)


def solve_sections(place, pieces, trace, y_left, z_high, z_low):
    quarters, rows, lanes = trace.shape
    height = rows // 2
    vmem, smem = (pl.BlockSpec(memory_space=space) for space in (pltpu.VMEM, pltpu.SMEM))
    flat = [array for section in pieces for kind in section for array in kind]
    parted = tuple(len(source) for source, _ in pieces)
    scratch = [
        pltpu.VMEM((quarters, rows, lanes), F32),
        pltpu.VMEM((2, quarters, 2, height + 2 * PAD, lanes), F32),
        pltpu.VMEM((quarters, 2, height, lanes), F32),
        pltpu.VMEM((quarters, 2, 2, height, lanes), BF16),
        pltpu.VMEM((quarters, rows, lanes), BF16),
        pltpu.VMEM((quarters, rows, lanes), BF16),
    ]
    inputs = flat + [trace, y_left, z_high, z_low]
    held = sum(a.size * a.dtype.itemsize for a in inputs + [trace])
    held += 8 * trace.size * trace.dtype.itemsize
    return pl.pallas_call(
        functools.partial(section_kernel, parted),
        out_shape=jax.ShapeDtypeStruct(trace.shape, F32),
        in_specs=[smem] + [vmem] * (len(flat) + 4),
        out_specs=vmem,
        scratch_shapes=scratch,
        compiler_params=pltpu.CompilerParams(vmem_limit_bytes=held + SPARE),
    )(place, *flat, trace, y_left, z_high, z_low)


def local(source, medium, damping, inv_x, inv_y, inv_z):
    rhs, _, height, lanes = source.shape[1:]
    sections, chips, cores = (lax.axis_size(a) for a in ("sec", "pen", "rhs"))
    pen, core = lax.axis_index("pen"), lax.axis_index("rhs")
    total = rhs * cores

    def owner(chip):
        return (chip % total) // rhs

    options = jnp.concatenate(
        [source[:, :, 0].swapaxes(0, 1), jnp.concatenate([medium, damping])[None]]
    ).reshape(rhs + 1, 2 * height, lanes)
    scale = jnp.broadcast_to(inv_x, (8, lanes))

    def message(distance):
        target = pen ^ distance
        pick = jnp.where(owner(target) == core, (target % total) % rhs, rhs)
        body = lax.dynamic_index_in_dim(options, pick, keepdims=False)
        return jnp.concatenate([body, scale])

    def between(value, down, from_owner):
        pairs = []
        for j in range(sections - down):
            for p in range(chips):
                here = owner(p) if from_owner else (owner(p) + 1) % cores
                pairs.append(
                    (
                        (j * chips + p) * cores + here,
                        ((j + down) * chips + p) * cores + owner(p),
                    )
                )
        return lax.ppermute(value, ("sec", "pen", "rhs"), pairs)

    y_high, y_low = split(CORNER * inv_y)
    y_left = jnp.concatenate(
        [jnp.concatenate([y_high, y_high], axis=2), jnp.concatenate([y_low, y_low], axis=2)],
        axis=1,
    )
    z_high, z_low = split(CORNER * inv_z.swapaxes(1, 2))
    place = pen ^ jnp.arange(chips, dtype=jnp.int32)

    got = [message(0)]
    for d in range(1, chips):
        got.append(lax.ppermute(message(d), "pen", [(i, i ^ d) for i in range(chips)]))
    middle = chips // 2
    near, y_left, z_high, z_low = lax.optimization_barrier(
        (jnp.stack(got[:middle]), y_left, z_high, z_low)
    )
    far = jnp.stack(got[middle:])

    arrived = [([], []) for _ in range(sections)]
    for value in (near, far):
        for k in range(sections - 1, 0, -1):
            for kind in range(2):
                arrived[k][kind].append(between(value, k, kind == 0))
    for value in (near, far):
        arrived[0][0].append(value)
        arrived[0][1].append(between(value, 0, False))
    head, rest = arrived[-1], arrived[-2::-1]

    fields = jnp.zeros((chips, 2 * height, lanes), F32)
    fields = solve_sections(place, [head], fields, y_left, z_high, z_low)
    fields = solve_sections(place, rest, fields, y_left, z_high, z_low)

    result = jnp.zeros((rhs, 2 * height, lanes), F32)
    for d in range(total):
        piece = lax.dynamic_index_in_dim(fields, pen ^ d, keepdims=False)
        if d > 0:
            pairs = [
                (i * cores + owner(i), (i ^ d) * cores + owner(i)) for i in range(chips)
            ]
            piece = lax.ppermute(piece, ("pen", "rhs"), pairs)
        origin = (pen ^ d) % total
        slot = (jnp.arange(rhs)[:, None, None] == origin % rhs) & (origin // rhs == core)
        result = jnp.where(slot, piece[None], result)
    return result.reshape(rhs, 2, height, lanes).swapaxes(0, 1)[:, :, None]


def solution(mesh):
    return jax.shard_map(
        local,
        mesh=mesh,
        in_specs=(
            P(None, "rhs", "sec", None, "pen"),
            P("sec", None, "pen"),
            P("sec", None, "pen"),
            P("sec", None),
            P(),
            P(),
        ),
        out_specs=P(None, "rhs", "sec", None, "pen"),
        check_vma=False,
    )
```

profile of v0, /device:TPU:0, one launch (start us, length us, event | category | flops | bytes accessed | tf_op | source)
XLA Modules:
  0.0 83.8 jit_solution(7523951287381906039)
XLA Ops:
  0.0 0.0 copy-start.3
  0.0 0.9 %copy-done.3 = f32[2,2,1,128,128]{4,3,2,1,0:T(8,128)S(1)} copy-done((f32[2,2,1,128,128]{4,3,2,1,0:T(8,128)S(1)}, f32[2,2,1,128,128]{4,3,2,1,0:T(8,128)}, u32[]{:S(2)}) %copy-start.3) | copy-done | bytes 262168
  1.0 0.0 copy-start.5
  1.0 0.0 copy-start.6
  1.7 0.1 copy-done.5
  1.8 0.0 copy-done.6
  1.9 0.1 fusion.8
  2.0 0.0 copy-start.2
  2.0 3.1 %collective-permute-start = (f32[264,128]{1,0:T(8,128)S(1)}, f32[264,128]{1,0:T(8,128)S(1)}, u32[]{:S(2)}, u32[]{:S(2)}) collective-permute-start(f32[264,128]{1,0:T(8,128)S(1)} %concatenate.37), channel_id=1, source_target_pairs={{0,2},{2,0},{4,6},{6,4},{1,3},{3,1},{5,7},{7,5},{8,10},{10,8},{12,... | collective-permute-start | bytes 405512 | tf_op jit(solution)/shard_map/ppermute | solution.py:265
  5.1 2.7 %collective-permute-start.2 = (f32[264,128]{1,0:T(8,128)S(1)}, f32[264,128]{1,0:T(8,128)S(1)}, u32[]{:S(2)}, u32[]{:S(2)}) collective-permute-start(f32[264,128]{1,0:T(8,128)S(1)} %concatenate.41), channel_id=1, source_target_pairs={{0,4},{2,6},{4,0},{6,2},{1,5},{3,7},{5,1},{7,3},{8,12},{10,14},{12... | collective-permute-start | bytes 405512 | tf_op jit(solution)/shard_map/ppermute | solution.py:265
  7.8 0.0 copy-start.4
  7.8 0.1 collective-permute-start.3
  7.9 0.7 copy-done.4
  8.7 0.0 copy-done.2
  8.7 0.2 copy.9
  8.9 0.1 fusion
  9.0 1.4 %collective-permute-done = f32[264,128]{1,0:T(8,128)S(1)} collective-permute-done((f32[264,128]{1,0:T(8,128)S(1)}, f32[264,128]{1,0:T(8,128)S(1)}, u32[]{:S(2)}, u32[]{:S(2)}) %collective-permute-start) | collective-permute-done | bytes 135200 | tf_op jit(solution)/shard_map/ppermute | solution.py:265
  10.4 4.6 %collective-permute-start.13 = (f32[2,264,128]{2,1,0:T(8,128)S(1)}, f32[2,264,128]{2,1,0:T(8,128)S(1)}, u32[]{:S(2)}, u32[]{:S(2)}) collective-permute-start(f32[2,264,128]{2,1,0:T(8,128)S(1)} %pad_maximum_fusion.refs_8_), channel_id=1, source_target_pairs={{0,24},{2,26},{5,29},{7,31}} | collective-permute-start | bytes 811016 | tf_op jit(solution)/shard_map/ppermute | solution.py:253
  15.0 0.7 collective-permute-start.15
  15.7 2.7 %collective-permute-done.2 = f32[264,128]{1,0:T(8,128)S(1)} collective-permute-done((f32[264,128]{1,0:T(8,128)S(1)}, f32[264,128]{1,0:T(8,128)S(1)}, u32[]{:S(2)}, u32[]{:S(2)}) %collective-permute-start.2) | collective-permute-done | bytes 135200 | tf_op jit(solution)/shard_map/ppermute | solution.py:265
  18.4 0.0 collective-permute-done.3
  18.4 4.4 %collective-permute-start.14 = (f32[2,264,128]{2,1,0:T(8,128)S(1)}, f32[2,264,128]{2,1,0:T(8,128)S(1)}, u32[]{:S(2)}, u32[]{:S(2)}) collective-permute-start(f32[2,264,128]{2,1,0:T(8,128)S(1)} %pad_maximum_fusion.1.refs_9_), channel_id=1, source_target_pairs={{0,24},{2,26},{5,29},{7,31}} | collective-permute-start | bytes 811016 | tf_op jit(solution)/shard_map/ppermute | solution.py:253
  22.8 0.7 collective-permute-start.16
  23.5 1.3 %collective-permute-start.1 = (f32[2,264,128]{2,1,0:T(8,128)S(1)}, f32[2,264,128]{2,1,0:T(8,128)S(1)}, u32[]{:S(2)}, u32[]{:S(2)}) collective-permute-start(f32[2,264,128]{2,1,0:T(8,128)S(1)} %pad_maximum_fusion.refs_8_), channel_id=1, source_target_pairs={{0,16},{2,18},{5,21},{7,23},{8,24},{10,26},{13,29},{15,31}} | collective-permute-start | bytes 811016 | tf_op jit(solution)/shard_map/ppermute | solution.py:253
  24.8 0.0 collective-permute-done.13.refs_0_
  24.8 1.3 %collective-permute-start.11 = (f32[2,264,128]{2,1,0:T(8,128)S(1)}, f32[2,264,128]{2,1,0:T(8,128)S(1)}, u32[]{:S(2)}, u32[]{:S(2)}) collective-permute-start(f32[2,264,128]{2,1,0:T(8,128)S(1)} %pad_maximum_fusion.refs_8_), channel_id=1, source_target_pairs={{1,0},{3,2},{4,5},{6,7},{9,8},{11,10},{12,13},{14,15},{17,16},{19,... | collective-permute-start | bytes 811016 | tf_op jit(solution)/shard_map/ppermute | solution.py:253
  26.1 0.0 collective-permute-done.15.refs_2_
  26.1 0.7 collective-permute-start.5
  26.8 2.1 %collective-permute-done.14.refs_1_ = f32[2,264,128]{2,1,0:T(8,128)S(1)} collective-permute-done((f32[2,264,128]{2,1,0:T(8,128)S(1)}, f32[2,264,128]{2,1,0:T(8,128)S(1)}, u32[]{:S(2)}, u32[]{:S(2)}) %collective-permute-start.14) | collective-permute-done | bytes 270368 | tf_op jit(solution)/shard_map/ppermute | solution.py:253
  28.9 1.3 %collective-permute-start.7 = (f32[2,264,128]{2,1,0:T(8,128)S(1)}, f32[2,264,128]{2,1,0:T(8,128)S(1)}, u32[]{:S(2)}, u32[]{:S(2)}) collective-permute-start(f32[2,264,128]{2,1,0:T(8,128)S(1)} %pad_maximum_fusion.refs_8_), channel_id=1, source_target_pairs={{0,8},{2,10},{5,13},{7,15},{8,16},{10,18},{13,21},{15,23},{16,24},... | collective-permute-start | bytes 811016 | tf_op jit(solution)/shard_map/ppermute | solution.py:253
  30.2 0.0 collective-permute-done.16.refs_3_
  30.2 0.7 collective-permute-start.9
  30.9 0.0 collective-permute-done.1.refs_0_
  30.9 1.4 %collective-permute-start.10 = (f32[2,264,128]{2,1,0:T(8,128)S(1)}, f32[2,264,128]{2,1,0:T(8,128)}, u32[]{:S(2)}, u32[]{:S(2)}) collective-permute-start(f32[2,264,128]{2,1,0:T(8,128)S(1)} %pad_maximum_fusion.1.refs_9_), channel_id=1, source_target_pairs={{1,8},{3,10},{4,13},{6,15},{9,16},{11,18},{12,21},{14,23},{17,24},... | collective-permute-start | bytes 811016 | tf_op jit(solution)/shard_map/ppermute | solution.py:253
  32.3 0.0 collective-permute-done.11.refs_10_
  32.3 1.3 %collective-permute-start.12 = (f32[2,264,128]{2,1,0:T(8,128)S(1)}, f32[2,264,128]{2,1,0:T(8,128)}, u32[]{:S(2)}, u32[]{:S(2)}) collective-permute-start(f32[2,264,128]{2,1,0:T(8,128)S(1)} %pad_maximum_fusion.1.refs_9_), channel_id=1, source_target_pairs={{1,0},{3,2},{4,5},{6,7},{9,8},{11,10},{12,13},{14,15},{17,16},{19,... | collective-permute-start | bytes 811016 | tf_op jit(solution)/shard_map/ppermute | solution.py:253
  33.6 0.0 collective-permute-done.5.refs_2_
  33.6 7.8 %collective-permute-start.4 = (f32[2,264,128]{2,1,0:T(8,128)S(1)}, f32[2,264,128]{2,1,0:T(8,128)}, u32[]{:S(2)}, u32[]{:S(2)}) collective-permute-start(f32[2,264,128]{2,1,0:T(8,128)S(1)} %pad_maximum_fusion.1.refs_9_), channel_id=1, source_target_pairs={{0,16},{2,18},{5,21},{7,23},{8,24},{10,26},{13,29},{15,31}} | collective-permute-start | bytes 811016 | tf_op jit(solution)/shard_map/ppermute | solution.py:253
  41.4 0.0 collective-permute-done.7.refs_4_
  41.4 1.4 %collective-permute-start.6 = (f32[2,264,128]{2,1,0:T(8,128)S(1)}, f32[2,264,128]{2,1,0:T(8,128)}, u32[]{:S(2)}, u32[]{:S(2)}) collective-permute-start(f32[2,264,128]{2,1,0:T(8,128)S(1)} %pad_maximum_fusion.1.refs_9_), channel_id=1, source_target_pairs={{1,16},{3,18},{4,21},{6,23},{9,24},{11,26},{12,29},{14,31}} | collective-permute-start | bytes 811016 | tf_op jit(solution)/shard_map/ppermute | solution.py:253
  42.7 0.0 collective-permute-done.9.refs_6_
  42.7 0.0 copy-start
  42.7 0.7 copy-done
  43.5 5.7 %collective-permute-start.8 = (f32[2,264,128]{2,1,0:T(8,128)S(1)}, f32[2,264,128]{2,1,0:T(8,128)}, u32[]{:S(2)}, u32[]{:S(2)}) collective-permute-start(f32[2,264,128]{2,1,0:T(8,128)S(1)} %pad_maximum_fusion.1.refs_9_), channel_id=1, source_target_pairs={{0,8},{2,10},{5,13},{7,15},{8,16},{10,18},{13,21},{15,23},{16,24},... | collective-permute-start | bytes 811016 | tf_op jit(solution)/shard_map/ppermute | solution.py:253
  49.2 0.0 copy-start.1
  49.2 5.8 %shard_map.64.refs_12_ = f32[4,256,128]{2,1,0:T(8,128)S(1)} custom-call(s32[4]{0:T(128)S(1)} %iota_xor_fusion.place, f32[2,264,128]{2,1,0:T(8,128)S(1)} %collective-permute-done.13.refs_0_, f32[2,264,128]{2,1,0:T(8,128)S(1)} %collective-permute-done.14.refs_1_, f32[2,264,128]{2,1,0:T(8,128)S(1)} %collective-permute-done.15.refs_2_, ...), custom_call_target="tpu_custom_call" | custom-call | tf_op jit(solution)/shard_map/pallas_call | solution.py:212
  55.0 0.0 collective-permute-done.10.refs_7_
  55.0 0.0 collective-permute-done.12.refs_11_
  55.1 0.0 collective-permute-done.4.refs_1_
  55.1 0.0 collective-permute-done.6.refs_3_
  55.1 0.0 collective-permute-done.8.refs_5_
  55.1 0.0 copy-done.1
  55.1 17.0 %shard_map.65 = f32[4,256,128]{2,1,0:T(8,128)S(1)} custom-call(s32[4]{0:T(128)S(1)} %iota_xor_fusion.place, f32[2,264,128]{2,1,0:T(8,128)S(1)} %collective-permute-done.1.refs_0_, f32[2,264,128]{2,1,0:T(8,128)} %collective-permute-done.4.refs_1_, f32[2,264,128]{2,1,0:T(8,128)S(1)} %collective-permute-done.5.refs_2_, ...), custom_call_target="tpu_custom_call" | custom-call | tf_op jit(solution)/shard_map/pallas_call | solution.py:212
  72.2 1.3 %collective-permute-start.17 = (f32[256,128]{1,0:T(8,128)S(1)}, f32[256,128]{1,0:T(8,128)S(1)}, u32[]{:S(2)}, u32[]{:S(2)}) collective-permute-start(f32[256,128]{1,0:T(8,128)S(1)} %get-tuple-element.13), channel_id=1, source_target_pairs={{0,6},{2,4},{5,3},{7,1},{8,14},{10,12},{13,11},{15,9},{16,22},{18,... | collective-permute-start | bytes 393224 | tf_op jit(solution)/shard_map/ppermute | solution.py:293
  73.5 1.3 %collective-permute-start.18 = (f32[256,128]{1,0:T(8,128)S(1)}, f32[256,128]{1,0:T(8,128)S(1)}, u32[]{:S(2)}, u32[]{:S(2)}) collective-permute-start(f32[256,128]{1,0:T(8,128)S(1)} %get-tuple-element.16), channel_id=1, source_target_pairs={{0,4},{2,6},{5,1},{7,3},{8,12},{10,14},{13,9},{15,11},{16,20},{18,... | collective-permute-start | bytes 393224 | tf_op jit(solution)/shard_map/ppermute | solution.py:293
  74.8 4.0 %collective-permute-start.19 = (f32[256,128]{1,0:T(8,128)S(1)}, f32[256,128]{1,0:T(8,128)S(1)}, u32[]{:S(2)}, u32[]{:S(2)}) collective-permute-start(f32[256,128]{1,0:T(8,128)S(1)} %get-tuple-element.15), channel_id=1, source_target_pairs={{0,2},{2,0},{5,7},{7,5},{8,10},{10,8},{13,15},{15,13},{16,18},{18,... | collective-permute-start | bytes 393224 | tf_op jit(solution)/shard_map/ppermute | solution.py:293
  78.8 0.0 collective-permute-done.17
  78.8 0.0 collective-permute-done.18
  78.8 4.2 %collective-permute-done.19 = f32[256,128]{1,0:T(8,128)S(1)} collective-permute-done((f32[256,128]{1,0:T(8,128)S(1)}, f32[256,128]{1,0:T(8,128)S(1)}, u32[]{:S(2)}, u32[]{:S(2)}) %collective-permute-start.19) | collective-permute-done | bytes 131104 | tf_op jit(solution)/shard_map/ppermute | solution.py:293
  83.0 0.8 select_select_fusion
  (15 shorter events, 0.3 us)
Async XLA Ops:
  0.0 0.9 %copy-start.3 = (f32[2,2,1,128,128]{4,3,2,1,0:T(8,128)S(1)}, f32[2,2,1,128,128]{4,3,2,1,0:T(8,128)}, u32[]{:S(2)}) copy-start(f32[2,2,1,128,128]{4,3,2,1,0:T(8,128)} %param.6) | copy-start | bytes 786436
  1.0 0.8 %copy-start.5 = (f32[1,128,128]{2,1,0:T(8,128)S(1)}, f32[1,128,128]{2,1,0:T(8,128)}, u32[]{:S(2)}) copy-start(f32[1,128,128]{2,1,0:T(8,128)} %param.8) | copy-start | bytes 196612
  1.0 0.9 %copy-start.6 = (f32[1,128,128]{2,1,0:T(8,128)S(1)}, f32[1,128,128]{2,1,0:T(8,128)}, u32[]{:S(2)}) copy-start(f32[1,128,128]{2,1,0:T(8,128)} %param.7) | copy-start | bytes 196612
  2.0 6.7 %copy-start.2 = (f32[2,256,256]{2,1,0:T(8,128)S(1)}, f32[2,256,256]{2,1,0:T(8,128)}, u32[]{:S(2)}) copy-start(f32[2,256,256]{2,1,0:T(8,128)} %param.11) | copy-start | bytes 1572868
  2.0 8.3 %collective-permute-start = (f32[264,128]{1,0:T(8,128)S(1)}, f32[264,128]{1,0:T(8,128)S(1)}, u32[]{:S(2)}, u32[]{:S(2)}) collective-permute-start(f32[264,128]{1,0:T(8,128)S(1)} %concatenate.37), channel_id=1, source_target_pairs={{0,2},{2,0},{4,6},{6,4},{1,3},{3,1},{5,7},{7,5},{8,10},{10,8},{12,... | collective-permute-start | bytes 405512 | tf_op jit(solution)/shard_map/ppermute | solution.py:265
  5.1 13.2 %collective-permute-start.2 = (f32[264,128]{1,0:T(8,128)S(1)}, f32[264,128]{1,0:T(8,128)S(1)}, u32[]{:S(2)}, u32[]{:S(2)}) collective-permute-start(f32[264,128]{1,0:T(8,128)S(1)} %concatenate.41), channel_id=1, source_target_pairs={{0,4},{2,6},{4,0},{6,2},{1,5},{3,7},{5,1},{7,3},{8,12},{10,14},{12... | collective-permute-start | bytes 405512 | tf_op jit(solution)/shard_map/ppermute | solution.py:265
  7.8 0.8 %copy-start.4 = (f32[1,128,128]{2,1,0:T(8,128)S(1)}, f32[1,128,128]{2,1,0:T(8,128)}, u32[]{:S(2)}) copy-start(f32[1,128,128]{2,1,0:T(8,128)} %param.10) | copy-start | bytes 196612
  7.8 10.5 %collective-permute-start.3 = (f32[264,128]{1,0:T(8,128)S(1)}, f32[264,128]{1,0:T(8,128)S(1)}, u32[]{:S(2)}, u32[]{:S(2)}) collective-permute-start(f32[264,128]{1,0:T(8,128)S(1)} %concatenate.42), channel_id=1, source_target_pairs={{0,6},{2,4},{4,2},{6,0},{1,7},{3,5},{5,3},{7,1},{8,14},{10,12},{12... | collective-permute-start | bytes 405512 | tf_op jit(solution)/shard_map/ppermute | solution.py:265
  10.4 14.4 %collective-permute-start.13 = (f32[2,264,128]{2,1,0:T(8,128)S(1)}, f32[2,264,128]{2,1,0:T(8,128)S(1)}, u32[]{:S(2)}, u32[]{:S(2)}) collective-permute-start(f32[2,264,128]{2,1,0:T(8,128)S(1)} %pad_maximum_fusion.refs_8_), channel_id=1, source_target_pairs={{0,24},{2,26},{5,29},{7,31}} | collective-permute-start | bytes 811016 | tf_op jit(solution)/shard_map/ppermute | solution.py:253
  15.0 11.1 %collective-permute-start.15 = (f32[2,264,128]{2,1,0:T(8,128)S(1)}, f32[2,264,128]{2,1,0:T(8,128)S(1)}, u32[]{:S(2)}, u32[]{:S(2)}) collective-permute-start(f32[2,264,128]{2,1,0:T(8,128)S(1)} %pad_maximum_fusion.refs_8_), channel_id=1, source_target_pairs={{1,24},{3,26},{4,29},{6,31}} | collective-permute-start | bytes 811016 | tf_op jit(solution)/shard_map/ppermute | solution.py:253
  18.4 10.5 %collective-permute-start.14 = (f32[2,264,128]{2,1,0:T(8,128)S(1)}, f32[2,264,128]{2,1,0:T(8,128)S(1)}, u32[]{:S(2)}, u32[]{:S(2)}) collective-permute-start(f32[2,264,128]{2,1,0:T(8,128)S(1)} %pad_maximum_fusion.1.refs_9_), channel_id=1, source_target_pairs={{0,24},{2,26},{5,29},{7,31}} | collective-permute-start | bytes 811016 | tf_op jit(solution)/shard_map/ppermute | solution.py:253
  22.8 7.5 %collective-permute-start.16 = (f32[2,264,128]{2,1,0:T(8,128)S(1)}, f32[2,264,128]{2,1,0:T(8,128)S(1)}, u32[]{:S(2)}, u32[]{:S(2)}) collective-permute-start(f32[2,264,128]{2,1,0:T(8,128)S(1)} %pad_maximum_fusion.1.refs_9_), channel_id=1, source_target_pairs={{1,24},{3,26},{4,29},{6,31}} | collective-permute-start | bytes 811016 | tf_op jit(solution)/shard_map/ppermute | solution.py:253
  23.5 7.5 %collective-permute-start.1 = (f32[2,264,128]{2,1,0:T(8,128)S(1)}, f32[2,264,128]{2,1,0:T(8,128)S(1)}, u32[]{:S(2)}, u32[]{:S(2)}) collective-permute-start(f32[2,264,128]{2,1,0:T(8,128)S(1)} %pad_maximum_fusion.refs_8_), channel_id=1, source_target_pairs={{0,16},{2,18},{5,21},{7,23},{8,24},{10,26},{13,29},{15,31}} | collective-permute-start | bytes 811016 | tf_op jit(solution)/shard_map/ppermute | solution.py:253
  24.8 7.5 %collective-permute-start.11 = (f32[2,264,128]{2,1,0:T(8,128)S(1)}, f32[2,264,128]{2,1,0:T(8,128)S(1)}, u32[]{:S(2)}, u32[]{:S(2)}) collective-permute-start(f32[2,264,128]{2,1,0:T(8,128)S(1)} %pad_maximum_fusion.refs_8_), channel_id=1, source_target_pairs={{1,0},{3,2},{4,5},{6,7},{9,8},{11,10},{12,13},{14,15},{17,16},{19,... | collective-permute-start | bytes 811016 | tf_op jit(solution)/shard_map/ppermute | solution.py:253
  26.1 7.5 %collective-permute-start.5 = (f32[2,264,128]{2,1,0:T(8,128)S(1)}, f32[2,264,128]{2,1,0:T(8,128)S(1)}, u32[]{:S(2)}, u32[]{:S(2)}) collective-permute-start(f32[2,264,128]{2,1,0:T(8,128)S(1)} %pad_maximum_fusion.refs_8_), channel_id=1, source_target_pairs={{1,16},{3,18},{4,21},{6,23},{9,24},{11,26},{12,29},{14,31}} | collective-permute-start | bytes 811016 | tf_op jit(solution)/shard_map/ppermute | solution.py:253
  28.9 12.5 %collective-permute-start.7 = (f32[2,264,128]{2,1,0:T(8,128)S(1)}, f32[2,264,128]{2,1,0:T(8,128)S(1)}, u32[]{:S(2)}, u32[]{:S(2)}) collective-permute-start(f32[2,264,128]{2,1,0:T(8,128)S(1)} %pad_maximum_fusion.refs_8_), channel_id=1, source_target_pairs={{0,8},{2,10},{5,13},{7,15},{8,16},{10,18},{13,21},{15,23},{16,24},... | collective-permute-start | bytes 811016 | tf_op jit(solution)/shard_map/ppermute | solution.py:253
  30.2 12.5 %collective-permute-start.9 = (f32[2,264,128]{2,1,0:T(8,128)S(1)}, f32[2,264,128]{2,1,0:T(8,128)S(1)}, u32[]{:S(2)}, u32[]{:S(2)}) collective-permute-start(f32[2,264,128]{2,1,0:T(8,128)S(1)} %pad_maximum_fusion.refs_8_), channel_id=1, source_target_pairs={{1,8},{3,10},{4,13},{6,15},{9,16},{11,18},{12,21},{14,23},{17,24},... | collective-permute-start | bytes 811016 | tf_op jit(solution)/shard_map/ppermute | solution.py:253
  30.9 24.1 %collective-permute-start.10 = (f32[2,264,128]{2,1,0:T(8,128)S(1)}, f32[2,264,128]{2,1,0:T(8,128)}, u32[]{:S(2)}, u32[]{:S(2)}) collective-permute-start(f32[2,264,128]{2,1,0:T(8,128)S(1)} %pad_maximum_fusion.1.refs_9_), channel_id=1, source_target_pairs={{1,8},{3,10},{4,13},{6,15},{9,16},{11,18},{12,21},{14,23},{17,24},... | collective-permute-start | bytes 811016 | tf_op jit(solution)/shard_map/ppermute | solution.py:253
  32.3 22.7 %collective-permute-start.12 = (f32[2,264,128]{2,1,0:T(8,128)S(1)}, f32[2,264,128]{2,1,0:T(8,128)}, u32[]{:S(2)}, u32[]{:S(2)}) collective-permute-start(f32[2,264,128]{2,1,0:T(8,128)S(1)} %pad_maximum_fusion.1.refs_9_), channel_id=1, source_target_pairs={{1,0},{3,2},{4,5},{6,7},{9,8},{11,10},{12,13},{14,15},{17,16},{19,... | collective-permute-start | bytes 811016 | tf_op jit(solution)/shard_map/ppermute | solution.py:253
  33.6 21.4 %collective-permute-start.4 = (f32[2,264,128]{2,1,0:T(8,128)S(1)}, f32[2,264,128]{2,1,0:T(8,128)}, u32[]{:S(2)}, u32[]{:S(2)}) collective-permute-start(f32[2,264,128]{2,1,0:T(8,128)S(1)} %pad_maximum_fusion.1.refs_9_), channel_id=1, source_target_pairs={{0,16},{2,18},{5,21},{7,23},{8,24},{10,26},{13,29},{15,31}} | collective-permute-start | bytes 811016 | tf_op jit(solution)/shard_map/ppermute | solution.py:253
  41.4 13.7 %collective-permute-start.6 = (f32[2,264,128]{2,1,0:T(8,128)S(1)}, f32[2,264,128]{2,1,0:T(8,128)}, u32[]{:S(2)}, u32[]{:S(2)}) collective-permute-start(f32[2,264,128]{2,1,0:T(8,128)S(1)} %pad_maximum_fusion.1.refs_9_), channel_id=1, source_target_pairs={{1,16},{3,18},{4,21},{6,23},{9,24},{11,26},{12,29},{14,31}} | collective-permute-start | bytes 811016 | tf_op jit(solution)/shard_map/ppermute | solution.py:253
  42.7 0.7 copy-start
  43.5 11.6 %collective-permute-start.8 = (f32[2,264,128]{2,1,0:T(8,128)S(1)}, f32[2,264,128]{2,1,0:T(8,128)}, u32[]{:S(2)}, u32[]{:S(2)}) collective-permute-start(f32[2,264,128]{2,1,0:T(8,128)S(1)} %pad_maximum_fusion.1.refs_9_), channel_id=1, source_target_pairs={{0,8},{2,10},{5,13},{7,15},{8,16},{10,18},{13,21},{15,23},{16,24},... | collective-permute-start | bytes 811016 | tf_op jit(solution)/shard_map/ppermute | solution.py:253
  49.2 5.9 %copy-start.1 = (f32[2,264,128]{2,1,0:T(8,128)S(1)}, f32[2,264,128]{2,1,0:T(8,128)}, u32[]{:S(2)}) copy-start(f32[2,264,128]{2,1,0:T(8,128)} %copy-done) | copy-start | bytes 811012
  72.2 6.6 %collective-permute-start.17 = (f32[256,128]{1,0:T(8,128)S(1)}, f32[256,128]{1,0:T(8,128)S(1)}, u32[]{:S(2)}, u32[]{:S(2)}) collective-permute-start(f32[256,128]{1,0:T(8,128)S(1)} %get-tuple-element.13), channel_id=1, source_target_pairs={{0,6},{2,4},{5,3},{7,1},{8,14},{10,12},{13,11},{15,9},{16,22},{18,... | collective-permute-start | bytes 393224 | tf_op jit(solution)/shard_map/ppermute | solution.py:293
  73.5 5.4 %collective-permute-start.18 = (f32[256,128]{1,0:T(8,128)S(1)}, f32[256,128]{1,0:T(8,128)S(1)}, u32[]{:S(2)}, u32[]{:S(2)}) collective-permute-start(f32[256,128]{1,0:T(8,128)S(1)} %get-tuple-element.16), channel_id=1, source_target_pairs={{0,4},{2,6},{5,1},{7,3},{8,12},{10,14},{13,9},{15,11},{16,20},{18,... | collective-permute-start | bytes 393224 | tf_op jit(solution)/shard_map/ppermute | solution.py:293
  74.8 8.2 %collective-permute-start.19 = (f32[256,128]{1,0:T(8,128)S(1)}, f32[256,128]{1,0:T(8,128)S(1)}, u32[]{:S(2)}, u32[]{:S(2)}) collective-permute-start(f32[256,128]{1,0:T(8,128)S(1)} %get-tuple-element.15), channel_id=1, source_target_pairs={{0,2},{2,0},{5,7},{7,5},{8,10},{10,8},{13,15},{15,13},{16,18},{18,... | collective-permute-start | bytes 393224 | tf_op jit(solution)/shard_map/ppermute | solution.py:293
where the time goes:
time: 84.3 us; the launch traced here: 83.8 us
  starting transfers between devices  45.5 us (54%)
  Pallas kernels  22.8 us (27%)
  waiting for transfers between devices  10.4 us (12%)
  local copies, waits for them, and re-layouts  2.91 us (3%)
  other arithmetic  1.12 us (1%)
  between operations  1.06 us (1%)
    ppermute x14, starting transfers between devices, between(): return lax.ppermute(value, ('sec', 'pen', 'rhs'), pairs)  33 us
    pallas_call x2, Pallas kernels, solve_sections(): pl.pallas_call(functools.partial(section_kernel, parted), out_shape=jax.S...  22.8 us
    ppermute x3, starting transfers between devices, local(): piece = lax.ppermute(piece, ('pen', 'rhs'), pairs)  6.59 us
    ppermute x3, starting transfers between devices, local(): lax.ppermute(message(d), 'pen', [(i, i ^ d) for i in range(chips)])  5.84 us
    ppermute x3, waiting for transfers between devices, local(): piece = lax.ppermute(piece, ('pen', 'rhs'), pairs)  4.16 us
    ppermute x3, waiting for transfers between devices, local(): lax.ppermute(message(d), 'pen', [(i, i ^ d) for i in range(chips)])  4.06 us
    unnamed x16, local copies, waits for them, and re-layouts  2.78 us
    ppermute x14, waiting for transfers between devices, between(): return lax.ppermute(value, ('sec', 'pen', 'rhs'), pairs)  2.18 us
  transfers between devices with their start and end apart: 20, of which 4 were waited for; matrix products, arithmetic and copies ran while one was open for 1% of the time, Pallas kernels for 7%

commit v1 on v0

--- a/solution.py
+++ b/solution.py
@@ -161,9 +161,9 @@
                             c * height : (c + 1) * height
                         ]
 
-    for index, (source, diagonal) in enumerate(pieces):
+    def solve(source, diagonal, before):
         gain = CORNER * source[0][0, 2 * height, :][None, :]
-        load(source, diagonal, trace if index == 0 else out, gain)
+        load(source, diagonal, before, gain)
         for q in range(quarters):
             out[q] = jnp.zeros(out.shape[1:], F32)
 
@@ -190,6 +190,19 @@
 
         lax.fori_loop(0, ITERS, sweep, 0)
         solve_z(True)
+
+    for index, (source, diagonal) in enumerate(pieces):
+        held = place[quarters + index] == 1
+        before = trace if index == 0 else out
+
+        @pl.when(held)
+        def _(source=source, diagonal=diagonal, before=before):
+            solve(source, diagonal, before)
+
+        @pl.when(jnp.logical_not(held))
+        def _():
+            for q in range(quarters):
+                out[q] = jnp.zeros(out.shape[1:], F32)
 
 
 def solve_sections(place, pieces, trace, y_left, z_high, z_low):
@@ -258,7 +271,12 @@
         axis=1,
     )
     z_high, z_low = split(CORNER * inv_z.swapaxes(1, 2))
-    place = pen ^ jnp.arange(chips, dtype=jnp.int32)
+    section, solver = lax.axis_index("sec"), owner(pen) == core
+
+    def place(downs):
+        held = jnp.stack([(section >= k) & solver for k in downs]).astype(jnp.int32)
+        return jnp.concatenate([pen ^ jnp.arange(chips, dtype=jnp.int32), held])
+
 
     got = [message(0)]
     for d in range(1, chips):
@@ -277,11 +295,14 @@
     for value in (near, far):
         arrived[0][0].append(value)
         arrived[0][1].append(between(value, 0, False))
-    head, rest = arrived[-1], arrived[-2::-1]
 
     fields = jnp.zeros((chips, 2 * height, lanes), F32)
-    fields = solve_sections(place, [head], fields, y_left, z_high, z_low)
-    fields = solve_sections(place, rest, fields, y_left, z_high, z_low)
+    downs = list(range(sections - 1, -1, -1))
+    for group in (downs[:1], downs[1:2], downs[2:]):
+        if group:
+            fields = solve_sections(
+                place(group), [arrived[k] for k in group], fields, y_left, z_high, z_low
+            )
 
     result = jnp.zeros((rhs, 2 * height, lanes), F32)
     for d in range(total):

time: 84.3 us -> 80.2 us (0.951)
  the two profiles are of different devices: /device:TPU:0 before, /device:TPU:14 now
where the time goes in v1:
time: 80.2 us; the launch traced here: 79.7 us
  starting transfers between devices  26.2 us (33%)
  waiting for transfers between devices  25.3 us (32%)
  Pallas kernels  23.9 us (30%)
  local copies, waits for them, and re-layouts  1.76 us (2%)
  other arithmetic  1.35 us (2%)
  between operations  1.09 us (1%)
    pallas_call x3, Pallas kernels, solve_sections(): pl.pallas_call(functools.partial(section_kernel, parted), out_shape=jax.S...  23.9 us
    ppermute x14, starting transfers between devices, between(): return lax.ppermute(value, ('sec', 'pen', 'rhs'), pairs)  18 us
    ppermute x14, waiting for transfers between devices, between(): return lax.ppermute(value, ('sec', 'pen', 'rhs'), pairs)  12 us
    ppermute x3, waiting for transfers between devices, local(): lax.ppermute(message(d), 'pen', [(i, i ^ d) for i in range(chips)])  8.38 us
    ppermute x3, waiting for transfers between devices, local(): piece = lax.ppermute(piece, ('pen', 'rhs'), pairs)  4.9 us
    ppermute x3, starting transfers between devices, local(): piece = lax.ppermute(piece, ('pen', 'rhs'), pairs)  4.52 us
    ppermute x3, starting transfers between devices, local(): lax.ppermute(message(d), 'pen', [(i, i ^ d) for i in range(chips)])  3.68 us
    unnamed x12, local copies, waits for them, and re-layouts  1.64 us
  transfers between devices with their start and end apart: 20, of which 9 were waited for; matrix products, arithmetic and copies ran while one was open for 1% of the time, Pallas kernels for 15%

profile of v1, /device:TPU:14, one launch (start us, length us, event | category | flops | bytes accessed | tf_op | source)
XLA Modules:
  0.0 79.7 jit_solution(9123903916430301850)
XLA Ops:
  0.0 0.0 copy-start.1
  0.0 0.9 %copy-done.1 = f32[2,2,1,128,128]{4,3,2,1,0:T(8,128)S(1)} copy-done((f32[2,2,1,128,128]{4,3,2,1,0:T(8,128)S(1)}, f32[2,2,1,128,128]{4,3,2,1,0:T(8,128)}, u32[]{:S(2)}) %copy-start.1) | copy-done | bytes 262168
  1.0 0.0 copy-start.3
  1.0 0.0 copy-start.4
  1.7 0.1 copy-done.3
  1.8 0.0 copy-done.4
  1.9 0.1 fusion.8
  2.0 0.0 copy-start
  2.0 0.5 collective-permute-start
  2.5 2.7 %collective-permute-start.2 = (f32[264,128]{1,0:T(8,128)S(1)}, f32[264,128]{1,0:T(8,128)S(1)}, u32[]{:S(2)}, u32[]{:S(2)}) collective-permute-start(f32[264,128]{1,0:T(8,128)S(1)} %concatenate.51), channel_id=1, source_target_pairs={{0,4},{2,6},{4,0},{6,2},{1,5},{3,7},{5,1},{7,3},{8,12},{10,14},{12... | collective-permute-start | bytes 405512 | tf_op jit(solution)/shard_map/ppermute | solution.py:283
  5.2 0.0 copy-start.2
  5.2 0.5 collective-permute-start.3
  5.7 0.3 copy-done.2
  6.1 0.0 copy-done
  6.1 0.2 copy.9
  6.3 0.1 fusion
  6.4 1.5 %collective-permute-done = f32[264,128]{1,0:T(8,128)S(1)} collective-permute-done((f32[264,128]{1,0:T(8,128)S(1)}, f32[264,128]{1,0:T(8,128)S(1)}, u32[]{:S(2)}, u32[]{:S(2)}) %collective-permute-start) | collective-permute-done | bytes 135200 | tf_op jit(solution)/shard_map/ppermute | solution.py:283
  7.9 1.3 %collective-permute-start.13 = (f32[2,264,128]{2,1,0:T(8,128)S(1)}, f32[2,264,128]{2,1,0:T(8,128)S(1)}, u32[]{:S(2)}, u32[]{:S(2)}) collective-permute-start(f32[2,264,128]{2,1,0:T(8,128)S(1)} %pad_maximum_fusion.refs_4_), channel_id=1, source_target_pairs={{0,24},{2,26},{5,29},{7,31}} | collective-permute-start | bytes 811016 | tf_op jit(solution)/shard_map/ppermute | solution.py:266
  9.2 1.3 %collective-permute-start.15 = (f32[2,264,128]{2,1,0:T(8,128)S(1)}, f32[2,264,128]{2,1,0:T(8,128)S(1)}, u32[]{:S(2)}, u32[]{:S(2)}) collective-permute-start(f32[2,264,128]{2,1,0:T(8,128)S(1)} %pad_maximum_fusion.refs_4_), channel_id=1, source_target_pairs={{1,24},{3,26},{4,29},{6,31}} | collective-permute-start | bytes 811016 | tf_op jit(solution)/shard_map/ppermute | solution.py:266
  10.5 4.2 %collective-permute-done.2 = f32[264,128]{1,0:T(8,128)S(1)} collective-permute-done((f32[264,128]{1,0:T(8,128)S(1)}, f32[264,128]{1,0:T(8,128)S(1)}, u32[]{:S(2)}, u32[]{:S(2)}) %collective-permute-start.2) | collective-permute-done | bytes 135200 | tf_op jit(solution)/shard_map/ppermute | solution.py:283
  14.8 2.6 %collective-permute-done.3 = f32[264,128]{1,0:T(8,128)S(1)} collective-permute-done((f32[264,128]{1,0:T(8,128)S(1)}, f32[264,128]{1,0:T(8,128)S(1)}, u32[]{:S(2)}, u32[]{:S(2)}) %collective-permute-start.3) | collective-permute-done | bytes 135200 | tf_op jit(solution)/shard_map/ppermute | solution.py:283
  17.4 1.3 %collective-permute-start.14 = (f32[2,264,128]{2,1,0:T(8,128)S(1)}, f32[2,264,128]{2,1,0:T(8,128)S(1)}, u32[]{:S(2)}, u32[]{:S(2)}) collective-permute-start(f32[2,264,128]{2,1,0:T(8,128)S(1)} %pad_maximum_fusion.1.refs_5_), channel_id=1, source_target_pairs={{0,24},{2,26},{5,29},{7,31}} | collective-permute-start | bytes 811016 | tf_op jit(solution)/shard_map/ppermute | solution.py:266
  18.7 1.3 %collective-permute-start.16 = (f32[2,264,128]{2,1,0:T(8,128)S(1)}, f32[2,264,128]{2,1,0:T(8,128)S(1)}, u32[]{:S(2)}, u32[]{:S(2)}) collective-permute-start(f32[2,264,128]{2,1,0:T(8,128)S(1)} %pad_maximum_fusion.1.refs_5_), channel_id=1, source_target_pairs={{1,24},{3,26},{4,29},{6,31}} | collective-permute-start | bytes 811016 | tf_op jit(solution)/shard_map/ppermute | solution.py:266
  20.0 1.3 %collective-permute-start.11 = (f32[2,264,128]{2,1,0:T(8,128)S(1)}, f32[2,264,128]{2,1,0:T(8,128)S(1)}, u32[]{:S(2)}, u32[]{:S(2)}) collective-permute-start(f32[2,264,128]{2,1,0:T(8,128)S(1)} %pad_maximum_fusion.refs_4_), channel_id=1, source_target_pairs={{1,16},{3,18},{4,21},{6,23},{9,24},{11,26},{12,29},{14,31}} | collective-permute-start | bytes 811016 | tf_op jit(solution)/shard_map/ppermute | solution.py:266
  21.3 0.0 collective-permute-done.13.refs_0_
  21.3 1.3 %collective-permute-start.9 = (f32[2,264,128]{2,1,0:T(8,128)S(1)}, f32[2,264,128]{2,1,0:T(8,128)S(1)}, u32[]{:S(2)}, u32[]{:S(2)}) collective-permute-start(f32[2,264,128]{2,1,0:T(8,128)S(1)} %pad_maximum_fusion.refs_4_), channel_id=1, source_target_pairs={{0,16},{2,18},{5,21},{7,23},{8,24},{10,26},{13,29},{15,31}} | collective-permute-start | bytes 811016 | tf_op jit(solution)/shard_map/ppermute | solution.py:266
  22.6 0.0 collective-permute-done.15.refs_2_
  22.7 1.3 %collective-permute-start.10 = (f32[2,264,128]{2,1,0:T(8,128)S(1)}, f32[2,264,128]{2,1,0:T(8,128)S(1)}, u32[]{:S(2)}, u32[]{:S(2)}) collective-permute-start(f32[2,264,128]{2,1,0:T(8,128)S(1)} %pad_maximum_fusion.1.refs_5_), channel_id=1, source_target_pairs={{0,16},{2,18},{5,21},{7,23},{8,24},{10,26},{13,29},{15,31}} | collective-permute-start | bytes 811016 | tf_op jit(solution)/shard_map/ppermute | solution.py:266
  24.0 5.0 %collective-permute-done.14.refs_1_ = f32[2,264,128]{2,1,0:T(8,128)S(1)} collective-permute-done((f32[2,264,128]{2,1,0:T(8,128)S(1)}, f32[2,264,128]{2,1,0:T(8,128)S(1)}, u32[]{:S(2)}, u32[]{:S(2)}) %collective-permute-start.14) | collective-permute-done | bytes 270368 | tf_op jit(solution)/shard_map/ppermute | solution.py:266
  29.0 1.3 %collective-permute-start.12 = (f32[2,264,128]{2,1,0:T(8,128)S(1)}, f32[2,264,128]{2,1,0:T(8,128)}, u32[]{:S(2)}, u32[]{:S(2)}) collective-permute-start(f32[2,264,128]{2,1,0:T(8,128)S(1)} %pad_maximum_fusion.1.refs_5_), channel_id=1, source_target_pairs={{1,16},{3,18},{4,21},{6,23},{9,24},{11,26},{12,29},{14,31}} | collective-permute-start | bytes 811016 | tf_op jit(solution)/shard_map/ppermute | solution.py:266
  30.2 0.0 collective-permute-done.16.refs_3_
  30.2 1.3 %collective-permute-start.1 = (f32[2,264,128]{2,1,0:T(8,128)S(1)}, f32[2,264,128]{2,1,0:T(8,128)S(1)}, u32[]{:S(2)}, u32[]{:S(2)}) collective-permute-start(f32[2,264,128]{2,1,0:T(8,128)S(1)} %pad_maximum_fusion.refs_4_), channel_id=1, source_target_pairs={{0,8},{2,10},{5,13},{7,15},{8,16},{10,18},{13,21},{15,23},{16,24},... | collective-permute-start | bytes 811016 | tf_op jit(solution)/shard_map/ppermute | solution.py:266
  31.6 3.7 %collective-permute-done.11.refs_2_ = f32[2,264,128]{2,1,0:T(8,128)S(1)} collective-permute-done((f32[2,264,128]{2,1,0:T(8,128)S(1)}, f32[2,264,128]{2,1,0:T(8,128)S(1)}, u32[]{:S(2)}, u32[]{:S(2)}) %collective-permute-start.11) | collective-permute-done | bytes 270368 | tf_op jit(solution)/shard_map/ppermute | solution.py:266
  35.3 1.3 %collective-permute-start.5 = (f32[2,264,128]{2,1,0:T(8,128)S(1)}, f32[2,264,128]{2,1,0:T(8,128)}, u32[]{:S(2)}, u32[]{:S(2)}) collective-permute-start(f32[2,264,128]{2,1,0:T(8,128)S(1)} %pad_maximum_fusion.refs_4_), channel_id=1, source_target_pairs={{1,8},{3,10},{4,13},{6,15},{9,16},{11,18},{12,21},{14,23},{17,24},... | collective-permute-start | bytes 811016 | tf_op jit(solution)/shard_map/ppermute | solution.py:266
  36.6 0.0 collective-permute-done.9.refs_0_
  36.6 1.3 %collective-permute-start.7 = (f32[2,264,128]{2,1,0:T(8,128)S(1)}, f32[2,264,128]{2,1,0:T(8,128)}, u32[]{:S(2)}, u32[]{:S(2)}) collective-permute-start(f32[2,264,128]{2,1,0:T(8,128)S(1)} %pad_maximum_fusion.refs_4_), channel_id=1, source_target_pairs={{1,0},{3,2},{4,5},{6,7},{9,8},{11,10},{12,13},{14,15},{17,16},{19,... | collective-permute-start | bytes 811016 | tf_op jit(solution)/shard_map/ppermute | solution.py:266
  37.9 3.3 %collective-permute-done.10.refs_1_ = f32[2,264,128]{2,1,0:T(8,128)S(1)} collective-permute-done((f32[2,264,128]{2,1,0:T(8,128)S(1)}, f32[2,264,128]{2,1,0:T(8,128)S(1)}, u32[]{:S(2)}, u32[]{:S(2)}) %collective-permute-start.10) | collective-permute-done | bytes 270368 | tf_op jit(solution)/shard_map/ppermute | solution.py:266
  41.2 1.3 %collective-permute-start.4 = (f32[2,264,128]{2,1,0:T(8,128)S(1)}, f32[2,264,128]{2,1,0:T(8,128)}, u32[]{:S(2)}, u32[]{:S(2)}) collective-permute-start(f32[2,264,128]{2,1,0:T(8,128)S(1)} %pad_maximum_fusion.1.refs_5_), channel_id=1, source_target_pairs={{0,8},{2,10},{5,13},{7,15},{8,16},{10,18},{13,21},{15,23},{16,24},... | collective-permute-start | bytes 811016 | tf_op jit(solution)/shard_map/ppermute | solution.py:266
  42.5 0.0 collective-permute-done.12.refs_3_
  42.5 1.3 %collective-permute-start.6 = (f32[2,264,128]{2,1,0:T(8,128)S(1)}, f32[2,264,128]{2,1,0:T(8,128)}, u32[]{:S(2)}, u32[]{:S(2)}) collective-permute-start(f32[2,264,128]{2,1,0:T(8,128)S(1)} %pad_maximum_fusion.1.refs_5_), channel_id=1, source_target_pairs={{1,8},{3,10},{4,13},{6,15},{9,16},{11,18},{12,21},{14,23},{17,24},... | collective-permute-start | bytes 811016 | tf_op jit(solution)/shard_map/ppermute | solution.py:266
  43.8 0.0 collective-permute-done.1.refs_0_
  43.8 1.3 %collective-permute-start.8 = (f32[2,264,128]{2,1,0:T(8,128)S(1)}, f32[2,264,128]{2,1,0:T(8,128)}, u32[]{:S(2)}, u32[]{:S(2)}) collective-permute-start(f32[2,264,128]{2,1,0:T(8,128)S(1)} %pad_maximum_fusion.1.refs_5_), channel_id=1, source_target_pairs={{1,0},{3,2},{4,5},{6,7},{9,8},{11,10},{12,13},{14,15},{17,16},{19,... | collective-permute-start | bytes 811016 | tf_op jit(solution)/shard_map/ppermute | solution.py:266
  45.1 0.1 add_convert_fusion
  45.2 0.1 pad_add_fusion.place
  45.2 0.1 pad_add_fusion.2
  45.4 5.8 %shard_map.64.refs_4_ = f32[4,256,128]{2,1,0:T(8,128)S(1)} custom-call(s32[5]{0:T(128)S(1)} %get-tuple-element.25.place, f32[2,264,128]{2,1,0:T(8,128)S(1)} %collective-permute-done.13.refs_0_, f32[2,264,128]{2,1,0:T(8,128)S(1)} %collective-permute-done.14.refs_1_, f32[2,264,128]{2,1,0:T(8,128)S(1)} %collective-permute-done.15.refs_2_, ...), custom_call_target="tpu_custom_call" | custom-call | tf_op jit(solution)/shard_map/pallas_call | solution.py:225
  51.2 6.2 %shard_map.65.refs_8_ = f32[4,256,128]{2,1,0:T(8,128)S(1)} custom-call(s32[5]{0:T(128)S(1)} %get-tuple-element.26.place, f32[2,264,128]{2,1,0:T(8,128)S(1)} %collective-permute-done.9.refs_0_, f32[2,264,128]{2,1,0:T(8,128)S(1)} %collective-permute-done.10.refs_1_, f32[2,264,128]{2,1,0:T(8,128)S(1)} %collective-permute-done.11.refs_2_, ...), custom_call_target="tpu_custom_call" | custom-call | tf_op jit(solution)/shard_map/pallas_call | solution.py:225
  57.4 0.0 collective-permute-done.5.refs_2_
  57.4 0.0 collective-permute-done.7.refs_6_
  57.5 0.0 collective-permute-done.4.refs_1_
  57.5 0.0 collective-permute-done.6.refs_3_
  57.5 0.0 collective-permute-done.8.refs_7_
  57.5 11.8 %shard_map.66 = f32[4,256,128]{2,1,0:T(8,128)S(1)} custom-call(s32[6]{0:T(128)S(1)} %pad_add_fusion.place, f32[2,264,128]{2,1,0:T(8,128)S(1)} %collective-permute-done.1.refs_0_, f32[2,264,128]{2,1,0:T(8,128)} %collective-permute-done.4.refs_1_, f32[2,264,128]{2,1,0:T(8,128)} %collective-permute-done.5.refs_2_, ...), custom_call_target="tpu_custom_call" | custom-call | tf_op jit(solution)/shard_map/pallas_call | solution.py:225
  69.4 1.3 %collective-permute-start.17 = (f32[256,128]{1,0:T(8,128)S(1)}, f32[256,128]{1,0:T(8,128)S(1)}, u32[]{:S(2)}, u32[]{:S(2)}) collective-permute-start(f32[256,128]{1,0:T(8,128)S(1)} %get-tuple-element.13), channel_id=1, source_target_pairs={{0,6},{2,4},{5,3},{7,1},{8,14},{10,12},{13,11},{15,9},{16,22},{18,... | collective-permute-start | bytes 393224 | tf_op jit(solution)/shard_map/ppermute | solution.py:314
  70.7 1.3 %collective-permute-start.18 = (f32[256,128]{1,0:T(8,128)S(1)}, f32[256,128]{1,0:T(8,128)S(1)}, u32[]{:S(2)}, u32[]{:S(2)}) collective-permute-start(f32[256,128]{1,0:T(8,128)S(1)} %get-tuple-element.16), channel_id=1, source_target_pairs={{0,4},{2,6},{5,1},{7,3},{8,12},{10,14},{13,9},{15,11},{16,20},{18,... | collective-permute-start | bytes 393224 | tf_op jit(solution)/shard_map/ppermute | solution.py:314
  72.0 1.9 %collective-permute-start.19 = (f32[256,128]{1,0:T(8,128)S(1)}, f32[256,128]{1,0:T(8,128)S(1)}, u32[]{:S(2)}, u32[]{:S(2)}) collective-permute-start(f32[256,128]{1,0:T(8,128)S(1)} %get-tuple-element.15), channel_id=1, source_target_pairs={{0,2},{2,0},{5,7},{7,5},{8,10},{10,8},{13,15},{15,13},{16,18},{18,... | collective-permute-start | bytes 393224 | tf_op jit(solution)/shard_map/ppermute | solution.py:314
  73.9 1.4 %collective-permute-done.17 = f32[256,128]{1,0:T(8,128)S(1)} collective-permute-done((f32[256,128]{1,0:T(8,128)S(1)}, f32[256,128]{1,0:T(8,128)S(1)}, u32[]{:S(2)}, u32[]{:S(2)}) %collective-permute-start.17) | collective-permute-done | bytes 131104 | tf_op jit(solution)/shard_map/ppermute | solution.py:314
  75.3 1.4 %collective-permute-done.18 = f32[256,128]{1,0:T(8,128)S(1)} collective-permute-done((f32[256,128]{1,0:T(8,128)S(1)}, f32[256,128]{1,0:T(8,128)S(1)}, u32[]{:S(2)}, u32[]{:S(2)}) %collective-permute-start.18) | collective-permute-done | bytes 131104 | tf_op jit(solution)/shard_map/ppermute | solution.py:314
  76.7 2.1 %collective-permute-done.19 = f32[256,128]{1,0:T(8,128)S(1)} collective-permute-done((f32[256,128]{1,0:T(8,128)S(1)}, f32[256,128]{1,0:T(8,128)S(1)}, u32[]{:S(2)}, u32[]{:S(2)}) %collective-permute-start.19) | collective-permute-done | bytes 131104 | tf_op jit(solution)/shard_map/ppermute | solution.py:314
  78.8 0.8 %select_select_fusion = f32[2,2,1,128,128]{4,3,2,1,0:T(8,128)} fusion(f32[2,128,128]{2,1,0:T(8,128)S(1)} %bitcast.43, f32[2,128,128]{2,1,0:T(8,128)S(1)} %bitcast.49, f32[2,128,128]{2,1,0:T(8,128)S(1)} %bitcast.48, f32[2,128,128]{2,1,0:T(8,128)S(1)} %bitcast.47, pred[2]{0:T(512)(128)(4,1)S(1)} %get-tuple-element.27, pred[2]{0:T(512)(128)(4,1)S(1)} %get-tuple-element.28, ...), kind=kLoop, calls=%fused_computation.13 | loop fusion | flops 262144 | bytes 786440 | tf_op jit(solution)/shard_map/jit(_where)/select_n | solution.py:317
  (15 shorter events, 0.3 us)
Async XLA Ops:
  0.0 0.9 %copy-start.1 = (f32[2,2,1,128,128]{4,3,2,1,0:T(8,128)S(1)}, f32[2,2,1,128,128]{4,3,2,1,0:T(8,128)}, u32[]{:S(2)}) copy-start(f32[2,2,1,128,128]{4,3,2,1,0:T(8,128)} %param.6) | copy-start | bytes 786436
  1.0 0.8 %copy-start.3 = (f32[1,128,128]{2,1,0:T(8,128)S(1)}, f32[1,128,128]{2,1,0:T(8,128)}, u32[]{:S(2)}) copy-start(f32[1,128,128]{2,1,0:T(8,128)} %param.8) | copy-start | bytes 196612
  1.0 0.9 %copy-start.4 = (f32[1,128,128]{2,1,0:T(8,128)S(1)}, f32[1,128,128]{2,1,0:T(8,128)}, u32[]{:S(2)}) copy-start(f32[1,128,128]{2,1,0:T(8,128)} %param.7) | copy-start | bytes 196612
  2.0 4.1 %copy-start = (f32[2,256,256]{2,1,0:T(8,128)S(1)}, f32[2,256,256]{2,1,0:T(8,128)}, u32[]{:S(2)}) copy-start(f32[2,256,256]{2,1,0:T(8,128)} %param.11) | copy-start | bytes 1572868
  2.0 5.9 %collective-permute-start = (f32[264,128]{1,0:T(8,128)S(1)}, f32[264,128]{1,0:T(8,128)S(1)}, u32[]{:S(2)}, u32[]{:S(2)}) collective-permute-start(f32[264,128]{1,0:T(8,128)S(1)} %concatenate.47), channel_id=1, source_target_pairs={{0,2},{2,0},{4,6},{6,4},{1,3},{3,1},{5,7},{7,5},{8,10},{10,8},{12,... | collective-permute-start | bytes 405512 | tf_op jit(solution)/shard_map/ppermute | solution.py:283
  2.5 12.2 %collective-permute-start.2 = (f32[264,128]{1,0:T(8,128)S(1)}, f32[264,128]{1,0:T(8,128)S(1)}, u32[]{:S(2)}, u32[]{:S(2)}) collective-permute-start(f32[264,128]{1,0:T(8,128)S(1)} %concatenate.51), channel_id=1, source_target_pairs={{0,4},{2,6},{4,0},{6,2},{1,5},{3,7},{5,1},{7,3},{8,12},{10,14},{12... | collective-permute-start | bytes 405512 | tf_op jit(solution)/shard_map/ppermute | solution.py:283
  5.2 0.8 %copy-start.2 = (f32[1,128,128]{2,1,0:T(8,128)S(1)}, f32[1,128,128]{2,1,0:T(8,128)}, u32[]{:S(2)}) copy-start(f32[1,128,128]{2,1,0:T(8,128)} %param.10) | copy-start | bytes 196612
  5.2 12.2 %collective-permute-start.3 = (f32[264,128]{1,0:T(8,128)S(1)}, f32[264,128]{1,0:T(8,128)S(1)}, u32[]{:S(2)}, u32[]{:S(2)}) collective-permute-start(f32[264,128]{1,0:T(8,128)S(1)} %concatenate.52), channel_id=1, source_target_pairs={{0,6},{2,4},{4,2},{6,0},{1,7},{3,5},{5,3},{7,1},{8,14},{10,12},{12... | collective-permute-start | bytes 405512 | tf_op jit(solution)/shard_map/ppermute | solution.py:283
  7.9 13.4 %collective-permute-start.13 = (f32[2,264,128]{2,1,0:T(8,128)S(1)}, f32[2,264,128]{2,1,0:T(8,128)S(1)}, u32[]{:S(2)}, u32[]{:S(2)}) collective-permute-start(f32[2,264,128]{2,1,0:T(8,128)S(1)} %pad_maximum_fusion.refs_4_), channel_id=1, source_target_pairs={{0,24},{2,26},{5,29},{7,31}} | collective-permute-start | bytes 811016 | tf_op jit(solution)/shard_map/ppermute | solution.py:266
  9.2 13.4 %collective-permute-start.15 = (f32[2,264,128]{2,1,0:T(8,128)S(1)}, f32[2,264,128]{2,1,0:T(8,128)S(1)}, u32[]{:S(2)}, u32[]{:S(2)}) collective-permute-start(f32[2,264,128]{2,1,0:T(8,128)S(1)} %pad_maximum_fusion.refs_4_), channel_id=1, source_target_pairs={{1,24},{3,26},{4,29},{6,31}} | collective-permute-start | bytes 811016 | tf_op jit(solution)/shard_map/ppermute | solution.py:266
  17.4 11.5 %collective-permute-start.14 = (f32[2,264,128]{2,1,0:T(8,128)S(1)}, f32[2,264,128]{2,1,0:T(8,128)S(1)}, u32[]{:S(2)}, u32[]{:S(2)}) collective-permute-start(f32[2,264,128]{2,1,0:T(8,128)S(1)} %pad_maximum_fusion.1.refs_5_), channel_id=1, source_target_pairs={{0,24},{2,26},{5,29},{7,31}} | collective-permute-start | bytes 811016 | tf_op jit(solution)/shard_map/ppermute | solution.py:266
  18.7 11.5 %collective-permute-start.16 = (f32[2,264,128]{2,1,0:T(8,128)S(1)}, f32[2,264,128]{2,1,0:T(8,128)S(1)}, u32[]{:S(2)}, u32[]{:S(2)}) collective-permute-start(f32[2,264,128]{2,1,0:T(8,128)S(1)} %pad_maximum_fusion.1.refs_5_), channel_id=1, source_target_pairs={{1,24},{3,26},{4,29},{6,31}} | collective-permute-start | bytes 811016 | tf_op jit(solution)/shard_map/ppermute | solution.py:266
  20.0 15.2 %collective-permute-start.11 = (f32[2,264,128]{2,1,0:T(8,128)S(1)}, f32[2,264,128]{2,1,0:T(8,128)S(1)}, u32[]{:S(2)}, u32[]{:S(2)}) collective-permute-start(f32[2,264,128]{2,1,0:T(8,128)S(1)} %pad_maximum_fusion.refs_4_), channel_id=1, source_target_pairs={{1,16},{3,18},{4,21},{6,23},{9,24},{11,26},{12,29},{14,31}} | collective-permute-start | bytes 811016 | tf_op jit(solution)/shard_map/ppermute | solution.py:266
  21.3 15.2 %collective-permute-start.9 = (f32[2,264,128]{2,1,0:T(8,128)S(1)}, f32[2,264,128]{2,1,0:T(8,128)S(1)}, u32[]{:S(2)}, u32[]{:S(2)}) collective-permute-start(f32[2,264,128]{2,1,0:T(8,128)S(1)} %pad_maximum_fusion.refs_4_), channel_id=1, source_target_pairs={{0,16},{2,18},{5,21},{7,23},{8,24},{10,26},{13,29},{15,31}} | collective-permute-start | bytes 811016 | tf_op jit(solution)/shard_map/ppermute | solution.py:266
  22.7 18.5 %collective-permute-start.10 = (f32[2,264,128]{2,1,0:T(8,128)S(1)}, f32[2,264,128]{2,1,0:T(8,128)S(1)}, u32[]{:S(2)}, u32[]{:S(2)}) collective-permute-start(f32[2,264,128]{2,1,0:T(8,128)S(1)} %pad_maximum_fusion.1.refs_5_), channel_id=1, source_target_pairs={{0,16},{2,18},{5,21},{7,23},{8,24},{10,26},{13,29},{15,31}} | collective-permute-start | bytes 811016 | tf_op jit(solution)/shard_map/ppermute | solution.py:266
  29.0 13.5 %collective-permute-start.12 = (f32[2,264,128]{2,1,0:T(8,128)S(1)}, f32[2,264,128]{2,1,0:T(8,128)}, u32[]{:S(2)}, u32[]{:S(2)}) collective-permute-start(f32[2,264,128]{2,1,0:T(8,128)S(1)} %pad_maximum_fusion.1.refs_5_), channel_id=1, source_target_pairs={{1,16},{3,18},{4,21},{6,23},{9,24},{11,26},{12,29},{14,31}} | collective-permute-start | bytes 811016 | tf_op jit(solution)/shard_map/ppermute | solution.py:266
  30.2 13.5 %collective-permute-start.1 = (f32[2,264,128]{2,1,0:T(8,128)S(1)}, f32[2,264,128]{2,1,0:T(8,128)S(1)}, u32[]{:S(2)}, u32[]{:S(2)}) collective-permute-start(f32[2,264,128]{2,1,0:T(8,128)S(1)} %pad_maximum_fusion.refs_4_), channel_id=1, source_target_pairs={{0,8},{2,10},{5,13},{7,15},{8,16},{10,18},{13,21},{15,23},{16,24},... | collective-permute-start | bytes 811016 | tf_op jit(solution)/shard_map/ppermute | solution.py:266
  35.3 22.2 %collective-permute-start.5 = (f32[2,264,128]{2,1,0:T(8,128)S(1)}, f32[2,264,128]{2,1,0:T(8,128)}, u32[]{:S(2)}, u32[]{:S(2)}) collective-permute-start(f32[2,264,128]{2,1,0:T(8,128)S(1)} %pad_maximum_fusion.refs_4_), channel_id=1, source_target_pairs={{1,8},{3,10},{4,13},{6,15},{9,16},{11,18},{12,21},{14,23},{17,24},... | collective-permute-start | bytes 811016 | tf_op jit(solution)/shard_map/ppermute | solution.py:266
  36.6 20.9 %collective-permute-start.7 = (f32[2,264,128]{2,1,0:T(8,128)S(1)}, f32[2,264,128]{2,1,0:T(8,128)}, u32[]{:S(2)}, u32[]{:S(2)}) collective-permute-start(f32[2,264,128]{2,1,0:T(8,128)S(1)} %pad_maximum_fusion.refs_4_), channel_id=1, source_target_pairs={{1,0},{3,2},{4,5},{6,7},{9,8},{11,10},{12,13},{14,15},{17,16},{19,... | collective-permute-start | bytes 811016 | tf_op jit(solution)/shard_map/ppermute | solution.py:266
  41.2 16.3 %collective-permute-start.4 = (f32[2,264,128]{2,1,0:T(8,128)S(1)}, f32[2,264,128]{2,1,0:T(8,128)}, u32[]{:S(2)}, u32[]{:S(2)}) collective-permute-start(f32[2,264,128]{2,1,0:T(8,128)S(1)} %pad_maximum_fusion.1.refs_5_), channel_id=1, source_target_pairs={{0,8},{2,10},{5,13},{7,15},{8,16},{10,18},{13,21},{15,23},{16,24},... | collective-permute-start | bytes 811016 | tf_op jit(solution)/shard_map/ppermute | solution.py:266
  42.5 15.0 %collective-permute-start.6 = (f32[2,264,128]{2,1,0:T(8,128)S(1)}, f32[2,264,128]{2,1,0:T(8,128)}, u32[]{:S(2)}, u32[]{:S(2)}) collective-permute-start(f32[2,264,128]{2,1,0:T(8,128)S(1)} %pad_maximum_fusion.1.refs_5_), channel_id=1, source_target_pairs={{1,8},{3,10},{4,13},{6,15},{9,16},{11,18},{12,21},{14,23},{17,24},... | collective-permute-start | bytes 811016 | tf_op jit(solution)/shard_map/ppermute | solution.py:266
  43.8 13.7 %collective-permute-start.8 = (f32[2,264,128]{2,1,0:T(8,128)S(1)}, f32[2,264,128]{2,1,0:T(8,128)}, u32[]{:S(2)}, u32[]{:S(2)}) collective-permute-start(f32[2,264,128]{2,1,0:T(8,128)S(1)} %pad_maximum_fusion.1.refs_5_), channel_id=1, source_target_pairs={{1,0},{3,2},{4,5},{6,7},{9,8},{11,10},{12,13},{14,15},{17,16},{19,... | collective-permute-start | bytes 811016 | tf_op jit(solution)/shard_map/ppermute | solution.py:266
  69.4 5.9 %collective-permute-start.17 = (f32[256,128]{1,0:T(8,128)S(1)}, f32[256,128]{1,0:T(8,128)S(1)}, u32[]{:S(2)}, u32[]{:S(2)}) collective-permute-start(f32[256,128]{1,0:T(8,128)S(1)} %get-tuple-element.13), channel_id=1, source_target_pairs={{0,6},{2,4},{5,3},{7,1},{8,14},{10,12},{13,11},{15,9},{16,22},{18,... | collective-permute-start | bytes 393224 | tf_op jit(solution)/shard_map/ppermute | solution.py:314
  70.7 6.0 %collective-permute-start.18 = (f32[256,128]{1,0:T(8,128)S(1)}, f32[256,128]{1,0:T(8,128)S(1)}, u32[]{:S(2)}, u32[]{:S(2)}) collective-permute-start(f32[256,128]{1,0:T(8,128)S(1)} %get-tuple-element.16), channel_id=1, source_target_pairs={{0,4},{2,6},{5,1},{7,3},{8,12},{10,14},{13,9},{15,11},{16,20},{18,... | collective-permute-start | bytes 393224 | tf_op jit(solution)/shard_map/ppermute | solution.py:314
  72.0 6.9 %collective-permute-start.19 = (f32[256,128]{1,0:T(8,128)S(1)}, f32[256,128]{1,0:T(8,128)S(1)}, u32[]{:S(2)}, u32[]{:S(2)}) collective-permute-start(f32[256,128]{1,0:T(8,128)S(1)} %get-tuple-element.15), channel_id=1, source_target_pairs={{0,2},{2,0},{5,7},{7,5},{8,10},{10,8},{13,15},{15,13},{16,18},{18,... | collective-permute-start | bytes 393224 | tf_op jit(solution)/shard_map/ppermute | solution.py:314

commit v2 on v1

--- a/solution.py
+++ b/solution.py
@@ -28,6 +28,15 @@
     return high.astype(BF16), (value - high).astype(BF16)
 
 
+def y_weights(blocks):
+    count, size, _ = blocks.shape
+    rows = [
+        jnp.concatenate([half, half], axis=2).reshape(count, size // ROWS, ROWS, 2 * size)
+        for half in split(blocks)
+    ]
+    return jnp.stack(rows, axis=2).reshape(count, 2 * size, 2 * size)
+
+
 def dot(a, b):
     return jnp.dot(a, b, preferred_element_type=F32)
 
@@ -35,7 +44,7 @@
 def section_kernel(parted, place, *refs):
     refs = list(refs)
     pieces = [[[refs.pop(0) for _ in range(n)] for _ in range(2)] for n in parted]
-    trace, y_left, z_high, z_low, out, res, step, diag, y_in, zh_in, zl_in = refs
+    trace, y_left, z_high, z_low, out, res, step, diag, y_in, z_in = refs
     parts, quarters, height, lanes = 2, res.shape[0], diag.shape[2], res.shape[2]
     y_blocks, y_size = y_left.shape[0], y_left.shape[1] // 2
     per_block = z_high.shape[1] // lanes
@@ -124,7 +133,8 @@
         y_in[q, c, 1, pl.ds(base, ROWS)] = low
 
     def for_z(q, c, base, rows, value):
-        zh_in[q, rows], zl_in[q, rows] = halves(value)
+        for h, part in enumerate(halves(value)):
+            z_in[q, pl.ds(base * 4 + (2 * h + c) * ROWS, ROWS)] = part
 
     def solve_y():
         for b in range(y_blocks):
@@ -139,27 +149,40 @@
                         axis=1,
                     )
                     done = dot(y_left[b], both)
-                    done = done[:y_size] + done[y_size:]
-                    for k in range(per_block):
-                        step[1, q + k, c, PAD + b * y_size : PAD + (b + 1) * y_size] = done[
-                            :, k * lanes : (k + 1) * lanes
-                        ]
+                    for i in range(y_size // ROWS):
+                        high, low = (
+                            done[(2 * i + h) * ROWS : (2 * i + h + 1) * ROWS] for h in range(2)
+                        )
+                        piece = high + low
+                        at = PAD + b * y_size + i * ROWS
+                        for k in range(per_block):
+                            step[1, q + k, c, at : at + ROWS] = piece[
+                                :, k * lanes : (k + 1) * lanes
+                            ]
 
     def solve_z(add):
         for b in range(quarters // per_block):
             span = range(b * per_block, (b + 1) * per_block)
-            high = jnp.concatenate([zh_in[q] for q in span], axis=1)
-            low = jnp.concatenate([zl_in[q] for q in span], axis=1)
-            done = dot(high, z_low[b]) + dot(low, z_high[b]) + dot(high, z_high[b])
-            for k, q in enumerate(span):
-                piece = done[:, k * lanes : (k + 1) * lanes]
-                if add:
-                    out[q] += piece
-                else:
-                    for c in range(parts):
-                        step[1, q, c, PAD : PAD + height] = piece[
-                            c * height : (c + 1) * height
-                        ]
+            both = jnp.concatenate([z_in[q] for q in span], axis=1)
+            group = 4 * ROWS
+            high = jnp.concatenate(
+                [both[i * group : i * group + 2 * ROWS] for i in range(chunks)], axis=0
+            )
+            main, rest = dot(both, z_high[b]), dot(high, z_low[b])
+            for i in range(chunks):
+                for c in range(parts):
+                    piece = rest[(2 * i + c) * ROWS : (2 * i + c + 1) * ROWS]
+                    for h in range(2):
+                        at = i * group + (2 * h + c) * ROWS
+                        piece = piece + main[at : at + ROWS]
+                    for k, q in enumerate(span):
+                        value = piece[:, k * lanes : (k + 1) * lanes]
+                        if add:
+                            at = c * height + i * ROWS
+                            out[q, at : at + ROWS] += value
+                        else:
+                            at = PAD + i * ROWS
+                            step[1, q, c, at : at + ROWS] = value
 
     def solve(source, diagonal, before):
         gain = CORNER * source[0][0, 2 * height, :][None, :]
@@ -216,8 +239,7 @@
         pltpu.VMEM((2, quarters, 2, height + 2 * PAD, lanes), F32),
         pltpu.VMEM((quarters, 2, height, lanes), F32),
         pltpu.VMEM((quarters, 2, 2, height, lanes), BF16),
-        pltpu.VMEM((quarters, rows, lanes), BF16),
-        pltpu.VMEM((quarters, rows, lanes), BF16),
+        pltpu.VMEM((quarters, 2 * rows, lanes), BF16),
     ]
     inputs = flat + [trace, y_left, z_high, z_low]
     held = sum(a.size * a.dtype.itemsize for a in inputs + [trace])
@@ -265,11 +287,7 @@
                 )
         return lax.ppermute(value, ("sec", "pen", "rhs"), pairs)
 
-    y_high, y_low = split(CORNER * inv_y)
-    y_left = jnp.concatenate(
-        [jnp.concatenate([y_high, y_high], axis=2), jnp.concatenate([y_low, y_low], axis=2)],
-        axis=1,
-    )
+    y_left = y_weights(CORNER * inv_y)
     z_high, z_low = split(CORNER * inv_z.swapaxes(1, 2))
     section, solver = lax.axis_index("sec"), owner(pen) == core
 

time: 80.2 us -> 79.9 us (level)
  no operation moved by 1% of the time
where the time goes in v2:
time: 79.9 us; the launch traced here: 79.4 us
  starting transfers between devices  26.2 us (33%)
  waiting for transfers between devices  25.3 us (32%)
  Pallas kernels  23.6 us (30%)
  local copies, waits for them, and re-layouts  1.76 us (2%)
  other arithmetic  1.37 us (2%)
  between operations  1.1 us (1%)
    pallas_call x3, Pallas kernels, solve_sections(): pl.pallas_call(functools.partial(section_kernel, parted), out_shape=jax.S...  23.6 us
    ppermute x14, starting transfers between devices, between(): return lax.ppermute(value, ('sec', 'pen', 'rhs'), pairs)  18 us
    ppermute x14, waiting for transfers between devices, between(): return lax.ppermute(value, ('sec', 'pen', 'rhs'), pairs)  12 us
    ppermute x3, waiting for transfers between devices, local(): lax.ppermute(message(d), 'pen', [(i, i ^ d) for i in range(chips)])  8.36 us
    ppermute x3, waiting for transfers between devices, local(): piece = lax.ppermute(piece, ('pen', 'rhs'), pairs)  4.9 us
    ppermute x3, starting transfers between devices, local(): piece = lax.ppermute(piece, ('pen', 'rhs'), pairs)  4.52 us
    ppermute x3, starting transfers between devices, local(): lax.ppermute(message(d), 'pen', [(i, i ^ d) for i in range(chips)])  3.68 us
    unnamed x12, local copies, waits for them, and re-layouts  1.64 us
  transfers between devices with their start and end apart: 20, of which 9 were waited for; matrix products, arithmetic and copies ran while one was open for 1% of the time, Pallas kernels for 15%

profile of v2, /device:TPU:14, one launch (start us, length us, event | category | flops | bytes accessed | tf_op | source)
XLA Modules:
  0.0 79.4 jit_solution(15790800465452877492)
XLA Ops:
  0.0 0.0 copy-start.1
  0.0 0.9 %copy-done.1 = f32[2,2,1,128,128]{4,3,2,1,0:T(8,128)S(1)} copy-done((f32[2,2,1,128,128]{4,3,2,1,0:T(8,128)S(1)}, f32[2,2,1,128,128]{4,3,2,1,0:T(8,128)}, u32[]{:S(2)}) %copy-start.1) | copy-done | bytes 262168
  1.0 0.0 copy-start.3
  1.0 0.0 copy-start.4
  1.7 0.1 copy-done.3
  1.8 0.0 copy-done.4
  1.9 0.1 fusion.8
  2.0 0.0 copy-start
  2.0 0.5 collective-permute-start
  2.5 2.7 %collective-permute-start.2 = (f32[264,128]{1,0:T(8,128)S(1)}, f32[264,128]{1,0:T(8,128)S(1)}, u32[]{:S(2)}, u32[]{:S(2)}) collective-permute-start(f32[264,128]{1,0:T(8,128)S(1)} %concatenate.47), channel_id=1, source_target_pairs={{0,4},{2,6},{4,0},{6,2},{1,5},{3,7},{5,1},{7,3},{8,12},{10,14},{12... | collective-permute-start | bytes 405512 | tf_op jit(solution)/shard_map/ppermute | solution.py:301
  5.2 0.0 copy-start.2
  5.2 0.5 collective-permute-start.3
  5.7 0.3 copy-done.2
  6.1 0.0 copy-done
  6.1 0.2 copy.13
  6.3 0.1 fusion
  6.4 1.5 %collective-permute-done = f32[264,128]{1,0:T(8,128)S(1)} collective-permute-done((f32[264,128]{1,0:T(8,128)S(1)}, f32[264,128]{1,0:T(8,128)S(1)}, u32[]{:S(2)}, u32[]{:S(2)}) %collective-permute-start) | collective-permute-done | bytes 135200 | tf_op jit(solution)/shard_map/ppermute | solution.py:301
  7.9 1.3 %collective-permute-start.13 = (f32[2,264,128]{2,1,0:T(8,128)S(1)}, f32[2,264,128]{2,1,0:T(8,128)S(1)}, u32[]{:S(2)}, u32[]{:S(2)}) collective-permute-start(f32[2,264,128]{2,1,0:T(8,128)S(1)} %pad_maximum_fusion.refs_4_), channel_id=1, source_target_pairs={{0,24},{2,26},{5,29},{7,31}} | collective-permute-start | bytes 811016 | tf_op jit(solution)/shard_map/ppermute | solution.py:288
  9.2 1.3 %collective-permute-start.15 = (f32[2,264,128]{2,1,0:T(8,128)S(1)}, f32[2,264,128]{2,1,0:T(8,128)S(1)}, u32[]{:S(2)}, u32[]{:S(2)}) collective-permute-start(f32[2,264,128]{2,1,0:T(8,128)S(1)} %pad_maximum_fusion.refs_4_), channel_id=1, source_target_pairs={{1,24},{3,26},{4,29},{6,31}} | collective-permute-start | bytes 811016 | tf_op jit(solution)/shard_map/ppermute | solution.py:288
  10.5 4.2 %collective-permute-done.2 = f32[264,128]{1,0:T(8,128)S(1)} collective-permute-done((f32[264,128]{1,0:T(8,128)S(1)}, f32[264,128]{1,0:T(8,128)S(1)}, u32[]{:S(2)}, u32[]{:S(2)}) %collective-permute-start.2) | collective-permute-done | bytes 135200 | tf_op jit(solution)/shard_map/ppermute | solution.py:301
  14.8 2.6 %collective-permute-done.3 = f32[264,128]{1,0:T(8,128)S(1)} collective-permute-done((f32[264,128]{1,0:T(8,128)S(1)}, f32[264,128]{1,0:T(8,128)S(1)}, u32[]{:S(2)}, u32[]{:S(2)}) %collective-permute-start.3) | collective-permute-done | bytes 135200 | tf_op jit(solution)/shard_map/ppermute | solution.py:301
  17.4 1.3 %collective-permute-start.14 = (f32[2,264,128]{2,1,0:T(8,128)S(1)}, f32[2,264,128]{2,1,0:T(8,128)S(1)}, u32[]{:S(2)}, u32[]{:S(2)}) collective-permute-start(f32[2,264,128]{2,1,0:T(8,128)S(1)} %pad_maximum_fusion.1.refs_5_), channel_id=1, source_target_pairs={{0,24},{2,26},{5,29},{7,31}} | collective-permute-start | bytes 811016 | tf_op jit(solution)/shard_map/ppermute | solution.py:288
  18.7 1.3 %collective-permute-start.16 = (f32[2,264,128]{2,1,0:T(8,128)S(1)}, f32[2,264,128]{2,1,0:T(8,128)S(1)}, u32[]{:S(2)}, u32[]{:S(2)}) collective-permute-start(f32[2,264,128]{2,1,0:T(8,128)S(1)} %pad_maximum_fusion.1.refs_5_), channel_id=1, source_target_pairs={{1,24},{3,26},{4,29},{6,31}} | collective-permute-start | bytes 811016 | tf_op jit(solution)/shard_map/ppermute | solution.py:288
  20.0 1.3 %collective-permute-start.11 = (f32[2,264,128]{2,1,0:T(8,128)S(1)}, f32[2,264,128]{2,1,0:T(8,128)S(1)}, u32[]{:S(2)}, u32[]{:S(2)}) collective-permute-start(f32[2,264,128]{2,1,0:T(8,128)S(1)} %pad_maximum_fusion.refs_4_), channel_id=1, source_target_pairs={{1,16},{3,18},{4,21},{6,23},{9,24},{11,26},{12,29},{14,31}} | collective-permute-start | bytes 811016 | tf_op jit(solution)/shard_map/ppermute | solution.py:288
  21.3 0.0 collective-permute-done.13.refs_0_
  21.3 1.3 %collective-permute-start.9 = (f32[2,264,128]{2,1,0:T(8,128)S(1)}, f32[2,264,128]{2,1,0:T(8,128)S(1)}, u32[]{:S(2)}, u32[]{:S(2)}) collective-permute-start(f32[2,264,128]{2,1,0:T(8,128)S(1)} %pad_maximum_fusion.refs_4_), channel_id=1, source_target_pairs={{0,16},{2,18},{5,21},{7,23},{8,24},{10,26},{13,29},{15,31}} | collective-permute-start | bytes 811016 | tf_op jit(solution)/shard_map/ppermute | solution.py:288
  22.6 0.0 collective-permute-done.15.refs_2_
  22.7 1.3 %collective-permute-start.10 = (f32[2,264,128]{2,1,0:T(8,128)S(1)}, f32[2,264,128]{2,1,0:T(8,128)S(1)}, u32[]{:S(2)}, u32[]{:S(2)}) collective-permute-start(f32[2,264,128]{2,1,0:T(8,128)S(1)} %pad_maximum_fusion.1.refs_5_), channel_id=1, source_target_pairs={{0,16},{2,18},{5,21},{7,23},{8,24},{10,26},{13,29},{15,31}} | collective-permute-start | bytes 811016 | tf_op jit(solution)/shard_map/ppermute | solution.py:288
  24.0 5.0 %collective-permute-done.14.refs_1_ = f32[2,264,128]{2,1,0:T(8,128)S(1)} collective-permute-done((f32[2,264,128]{2,1,0:T(8,128)S(1)}, f32[2,264,128]{2,1,0:T(8,128)S(1)}, u32[]{:S(2)}, u32[]{:S(2)}) %collective-permute-start.14) | collective-permute-done | bytes 270368 | tf_op jit(solution)/shard_map/ppermute | solution.py:288
  29.0 1.3 %collective-permute-start.12 = (f32[2,264,128]{2,1,0:T(8,128)S(1)}, f32[2,264,128]{2,1,0:T(8,128)}, u32[]{:S(2)}, u32[]{:S(2)}) collective-permute-start(f32[2,264,128]{2,1,0:T(8,128)S(1)} %pad_maximum_fusion.1.refs_5_), channel_id=1, source_target_pairs={{1,16},{3,18},{4,21},{6,23},{9,24},{11,26},{12,29},{14,31}} | collective-permute-start | bytes 811016 | tf_op jit(solution)/shard_map/ppermute | solution.py:288
  30.2 0.0 collective-permute-done.16.refs_3_
  30.2 1.3 %collective-permute-start.1 = (f32[2,264,128]{2,1,0:T(8,128)S(1)}, f32[2,264,128]{2,1,0:T(8,128)S(1)}, u32[]{:S(2)}, u32[]{:S(2)}) collective-permute-start(f32[2,264,128]{2,1,0:T(8,128)S(1)} %pad_maximum_fusion.refs_4_), channel_id=1, source_target_pairs={{0,8},{2,10},{5,13},{7,15},{8,16},{10,18},{13,21},{15,23},{16,24},... | collective-permute-start | bytes 811016 | tf_op jit(solution)/shard_map/ppermute | solution.py:288
  31.6 3.7 %collective-permute-done.11.refs_2_ = f32[2,264,128]{2,1,0:T(8,128)S(1)} collective-permute-done((f32[2,264,128]{2,1,0:T(8,128)S(1)}, f32[2,264,128]{2,1,0:T(8,128)S(1)}, u32[]{:S(2)}, u32[]{:S(2)}) %collective-permute-start.11) | collective-permute-done | bytes 270368 | tf_op jit(solution)/shard_map/ppermute | solution.py:288
  35.3 1.3 %collective-permute-start.5 = (f32[2,264,128]{2,1,0:T(8,128)S(1)}, f32[2,264,128]{2,1,0:T(8,128)}, u32[]{:S(2)}, u32[]{:S(2)}) collective-permute-start(f32[2,264,128]{2,1,0:T(8,128)S(1)} %pad_maximum_fusion.refs_4_), channel_id=1, source_target_pairs={{1,8},{3,10},{4,13},{6,15},{9,16},{11,18},{12,21},{14,23},{17,24},... | collective-permute-start | bytes 811016 | tf_op jit(solution)/shard_map/ppermute | solution.py:288
  36.6 0.0 collective-permute-done.9.refs_0_
  36.6 1.3 %collective-permute-start.7 = (f32[2,264,128]{2,1,0:T(8,128)S(1)}, f32[2,264,128]{2,1,0:T(8,128)}, u32[]{:S(2)}, u32[]{:S(2)}) collective-permute-start(f32[2,264,128]{2,1,0:T(8,128)S(1)} %pad_maximum_fusion.refs_4_), channel_id=1, source_target_pairs={{1,0},{3,2},{4,5},{6,7},{9,8},{11,10},{12,13},{14,15},{17,16},{19,... | collective-permute-start | bytes 811016 | tf_op jit(solution)/shard_map/ppermute | solution.py:288
  37.9 3.3 %collective-permute-done.10.refs_1_ = f32[2,264,128]{2,1,0:T(8,128)S(1)} collective-permute-done((f32[2,264,128]{2,1,0:T(8,128)S(1)}, f32[2,264,128]{2,1,0:T(8,128)S(1)}, u32[]{:S(2)}, u32[]{:S(2)}) %collective-permute-start.10) | collective-permute-done | bytes 270368 | tf_op jit(solution)/shard_map/ppermute | solution.py:288
  41.2 1.3 %collective-permute-start.4 = (f32[2,264,128]{2,1,0:T(8,128)S(1)}, f32[2,264,128]{2,1,0:T(8,128)}, u32[]{:S(2)}, u32[]{:S(2)}) collective-permute-start(f32[2,264,128]{2,1,0:T(8,128)S(1)} %pad_maximum_fusion.1.refs_5_), channel_id=1, source_target_pairs={{0,8},{2,10},{5,13},{7,15},{8,16},{10,18},{13,21},{15,23},{16,24},... | collective-permute-start | bytes 811016 | tf_op jit(solution)/shard_map/ppermute | solution.py:288
  42.5 0.0 collective-permute-done.12.refs_3_
  42.5 1.3 %collective-permute-start.6 = (f32[2,264,128]{2,1,0:T(8,128)S(1)}, f32[2,264,128]{2,1,0:T(8,128)}, u32[]{:S(2)}, u32[]{:S(2)}) collective-permute-start(f32[2,264,128]{2,1,0:T(8,128)S(1)} %pad_maximum_fusion.1.refs_5_), channel_id=1, source_target_pairs={{1,8},{3,10},{4,13},{6,15},{9,16},{11,18},{12,21},{14,23},{17,24},... | collective-permute-start | bytes 811016 | tf_op jit(solution)/shard_map/ppermute | solution.py:288
  43.8 0.0 collective-permute-done.1.refs_0_
  43.8 1.3 %collective-permute-start.8 = (f32[2,264,128]{2,1,0:T(8,128)S(1)}, f32[2,264,128]{2,1,0:T(8,128)}, u32[]{:S(2)}, u32[]{:S(2)}) collective-permute-start(f32[2,264,128]{2,1,0:T(8,128)S(1)} %pad_maximum_fusion.1.refs_5_), channel_id=1, source_target_pairs={{1,0},{3,2},{4,5},{6,7},{9,8},{11,10},{12,13},{14,15},{17,16},{19,... | collective-permute-start | bytes 811016 | tf_op jit(solution)/shard_map/ppermute | solution.py:288
  45.1 0.1 add_convert_fusion
  45.2 0.1 pad_add_fusion.place
  45.2 0.1 pad_add_fusion.2
  45.4 5.7 %shard_map.64.refs_4_ = f32[4,256,128]{2,1,0:T(8,128)S(1)} custom-call(s32[5]{0:T(128)S(1)} %get-tuple-element.25.place, f32[2,264,128]{2,1,0:T(8,128)S(1)} %collective-permute-done.13.refs_0_, f32[2,264,128]{2,1,0:T(8,128)S(1)} %collective-permute-done.14.refs_1_, f32[2,264,128]{2,1,0:T(8,128)S(1)} %collective-permute-done.15.refs_2_, ...), custom_call_target="tpu_custom_call" | custom-call | tf_op jit(solution)/shard_map/pallas_call | solution.py:247
  51.1 6.2 %shard_map.65.refs_8_ = f32[4,256,128]{2,1,0:T(8,128)S(1)} custom-call(s32[5]{0:T(128)S(1)} %get-tuple-element.26.place, f32[2,264,128]{2,1,0:T(8,128)S(1)} %collective-permute-done.9.refs_0_, f32[2,264,128]{2,1,0:T(8,128)S(1)} %collective-permute-done.10.refs_1_, f32[2,264,128]{2,1,0:T(8,128)S(1)} %collective-permute-done.11.refs_2_, ...), custom_call_target="tpu_custom_call" | custom-call | tf_op jit(solution)/shard_map/pallas_call | solution.py:247
  57.3 0.0 collective-permute-done.5.refs_2_
  57.3 0.0 collective-permute-done.7.refs_6_
  57.3 0.0 collective-permute-done.4.refs_1_
  57.3 0.0 collective-permute-done.6.refs_3_
  57.3 0.0 collective-permute-done.8.refs_7_
  57.3 11.7 %shard_map.66 = f32[4,256,128]{2,1,0:T(8,128)S(1)} custom-call(s32[6]{0:T(128)S(1)} %pad_add_fusion.place, f32[2,264,128]{2,1,0:T(8,128)S(1)} %collective-permute-done.1.refs_0_, f32[2,264,128]{2,1,0:T(8,128)} %collective-permute-done.4.refs_1_, f32[2,264,128]{2,1,0:T(8,128)} %collective-permute-done.5.refs_2_, ...), custom_call_target="tpu_custom_call" | custom-call | tf_op jit(solution)/shard_map/pallas_call | solution.py:247
  69.1 1.3 %collective-permute-start.17 = (f32[256,128]{1,0:T(8,128)S(1)}, f32[256,128]{1,0:T(8,128)S(1)}, u32[]{:S(2)}, u32[]{:S(2)}) collective-permute-start(f32[256,128]{1,0:T(8,128)S(1)} %get-tuple-element.13), channel_id=1, source_target_pairs={{0,6},{2,4},{5,3},{7,1},{8,14},{10,12},{13,11},{15,9},{16,22},{18,... | collective-permute-start | bytes 393224 | tf_op jit(solution)/shard_map/ppermute | solution.py:332
  70.4 1.3 %collective-permute-start.18 = (f32[256,128]{1,0:T(8,128)S(1)}, f32[256,128]{1,0:T(8,128)S(1)}, u32[]{:S(2)}, u32[]{:S(2)}) collective-permute-start(f32[256,128]{1,0:T(8,128)S(1)} %get-tuple-element.16), channel_id=1, source_target_pairs={{0,4},{2,6},{5,1},{7,3},{8,12},{10,14},{13,9},{15,11},{16,20},{18,... | collective-permute-start | bytes 393224 | tf_op jit(solution)/shard_map/ppermute | solution.py:332
  71.7 1.9 %collective-permute-start.19 = (f32[256,128]{1,0:T(8,128)S(1)}, f32[256,128]{1,0:T(8,128)S(1)}, u32[]{:S(2)}, u32[]{:S(2)}) collective-permute-start(f32[256,128]{1,0:T(8,128)S(1)} %get-tuple-element.15), channel_id=1, source_target_pairs={{0,2},{2,0},{5,7},{7,5},{8,10},{10,8},{13,15},{15,13},{16,18},{18,... | collective-permute-start | bytes 393224 | tf_op jit(solution)/shard_map/ppermute | solution.py:332
  73.7 1.4 %collective-permute-done.17 = f32[256,128]{1,0:T(8,128)S(1)} collective-permute-done((f32[256,128]{1,0:T(8,128)S(1)}, f32[256,128]{1,0:T(8,128)S(1)}, u32[]{:S(2)}, u32[]{:S(2)}) %collective-permute-start.17) | collective-permute-done | bytes 131104 | tf_op jit(solution)/shard_map/ppermute | solution.py:332
  75.0 1.4 %collective-permute-done.18 = f32[256,128]{1,0:T(8,128)S(1)} collective-permute-done((f32[256,128]{1,0:T(8,128)S(1)}, f32[256,128]{1,0:T(8,128)S(1)}, u32[]{:S(2)}, u32[]{:S(2)}) %collective-permute-start.18) | collective-permute-done | bytes 131104 | tf_op jit(solution)/shard_map/ppermute | solution.py:332
  76.4 2.1 %collective-permute-done.19 = f32[256,128]{1,0:T(8,128)S(1)} collective-permute-done((f32[256,128]{1,0:T(8,128)S(1)}, f32[256,128]{1,0:T(8,128)S(1)}, u32[]{:S(2)}, u32[]{:S(2)}) %collective-permute-start.19) | collective-permute-done | bytes 131104 | tf_op jit(solution)/shard_map/ppermute | solution.py:332
  78.6 0.8 %select_select_fusion = f32[2,2,1,128,128]{4,3,2,1,0:T(8,128)} fusion(f32[2,128,128]{2,1,0:T(8,128)S(1)} %bitcast.53, f32[2,128,128]{2,1,0:T(8,128)S(1)} %bitcast.61, f32[2,128,128]{2,1,0:T(8,128)S(1)} %bitcast.60, f32[2,128,128]{2,1,0:T(8,128)S(1)} %bitcast.59, pred[2]{0:T(512)(128)(4,1)S(1)} %get-tuple-element.29, pred[2]{0:T(512)(128)(4,1)S(1)} %get-tuple-element.30, ...), kind=kLoop, calls=%fused_computation.13 | loop fusion | flops 262144 | bytes 786440 | tf_op jit(solution)/shard_map/jit(_where)/select_n | solution.py:335
  (16 shorter events, 0.3 us)
Async XLA Ops:
  0.0 0.9 %copy-start.1 = (f32[2,2,1,128,128]{4,3,2,1,0:T(8,128)S(1)}, f32[2,2,1,128,128]{4,3,2,1,0:T(8,128)}, u32[]{:S(2)}) copy-start(f32[2,2,1,128,128]{4,3,2,1,0:T(8,128)} %param.6) | copy-start | bytes 786436
  1.0 0.8 %copy-start.3 = (f32[1,128,128]{2,1,0:T(8,128)S(1)}, f32[1,128,128]{2,1,0:T(8,128)}, u32[]{:S(2)}) copy-start(f32[1,128,128]{2,1,0:T(8,128)} %param.8) | copy-start | bytes 196612
  1.0 0.9 %copy-start.4 = (f32[1,128,128]{2,1,0:T(8,128)S(1)}, f32[1,128,128]{2,1,0:T(8,128)}, u32[]{:S(2)}) copy-start(f32[1,128,128]{2,1,0:T(8,128)} %param.7) | copy-start | bytes 196612
  2.0 4.1 %copy-start = (f32[2,256,256]{2,1,0:T(8,128)S(1)}, f32[2,256,256]{2,1,0:T(8,128)}, u32[]{:S(2)}) copy-start(f32[2,256,256]{2,1,0:T(8,128)} %param.11) | copy-start | bytes 1572868
  2.0 5.9 %collective-permute-start = (f32[264,128]{1,0:T(8,128)S(1)}, f32[264,128]{1,0:T(8,128)S(1)}, u32[]{:S(2)}, u32[]{:S(2)}) collective-permute-start(f32[264,128]{1,0:T(8,128)S(1)} %concatenate.44), channel_id=1, source_target_pairs={{0,2},{2,0},{4,6},{6,4},{1,3},{3,1},{5,7},{7,5},{8,10},{10,8},{12,... | collective-permute-start | bytes 405512 | tf_op jit(solution)/shard_map/ppermute | solution.py:301
  2.5 12.2 %collective-permute-start.2 = (f32[264,128]{1,0:T(8,128)S(1)}, f32[264,128]{1,0:T(8,128)S(1)}, u32[]{:S(2)}, u32[]{:S(2)}) collective-permute-start(f32[264,128]{1,0:T(8,128)S(1)} %concatenate.47), channel_id=1, source_target_pairs={{0,4},{2,6},{4,0},{6,2},{1,5},{3,7},{5,1},{7,3},{8,12},{10,14},{12... | collective-permute-start | bytes 405512 | tf_op jit(solution)/shard_map/ppermute | solution.py:301
  5.2 0.8 %copy-start.2 = (f32[1,128,128]{2,1,0:T(8,128)S(1)}, f32[1,128,128]{2,1,0:T(8,128)}, u32[]{:S(2)}) copy-start(f32[1,128,128]{2,1,0:T(8,128)} %param.10) | copy-start | bytes 196612
  5.2 12.2 %collective-permute-start.3 = (f32[264,128]{1,0:T(8,128)S(1)}, f32[264,128]{1,0:T(8,128)S(1)}, u32[]{:S(2)}, u32[]{:S(2)}) collective-permute-start(f32[264,128]{1,0:T(8,128)S(1)} %concatenate.48), channel_id=1, source_target_pairs={{0,6},{2,4},{4,2},{6,0},{1,7},{3,5},{5,3},{7,1},{8,14},{10,12},{12... | collective-permute-start | bytes 405512 | tf_op jit(solution)/shard_map/ppermute | solution.py:301
  7.9 13.4 %collective-permute-start.13 = (f32[2,264,128]{2,1,0:T(8,128)S(1)}, f32[2,264,128]{2,1,0:T(8,128)S(1)}, u32[]{:S(2)}, u32[]{:S(2)}) collective-permute-start(f32[2,264,128]{2,1,0:T(8,128)S(1)} %pad_maximum_fusion.refs_4_), channel_id=1, source_target_pairs={{0,24},{2,26},{5,29},{7,31}} | collective-permute-start | bytes 811016 | tf_op jit(solution)/shard_map/ppermute | solution.py:288
  9.2 13.4 %collective-permute-start.15 = (f32[2,264,128]{2,1,0:T(8,128)S(1)}, f32[2,264,128]{2,1,0:T(8,128)S(1)}, u32[]{:S(2)}, u32[]{:S(2)}) collective-permute-start(f32[2,264,128]{2,1,0:T(8,128)S(1)} %pad_maximum_fusion.refs_4_), channel_id=1, source_target_pairs={{1,24},{3,26},{4,29},{6,31}} | collective-permute-start | bytes 811016 | tf_op jit(solution)/shard_map/ppermute | solution.py:288
  17.4 11.5 %collective-permute-start.14 = (f32[2,264,128]{2,1,0:T(8,128)S(1)}, f32[2,264,128]{2,1,0:T(8,128)S(1)}, u32[]{:S(2)}, u32[]{:S(2)}) collective-permute-start(f32[2,264,128]{2,1,0:T(8,128)S(1)} %pad_maximum_fusion.1.refs_5_), channel_id=1, source_target_pairs={{0,24},{2,26},{5,29},{7,31}} | collective-permute-start | bytes 811016 | tf_op jit(solution)/shard_map/ppermute | solution.py:288
  18.7 11.5 %collective-permute-start.16 = (f32[2,264,128]{2,1,0:T(8,128)S(1)}, f32[2,264,128]{2,1,0:T(8,128)S(1)}, u32[]{:S(2)}, u32[]{:S(2)}) collective-permute-start(f32[2,264,128]{2,1,0:T(8,128)S(1)} %pad_maximum_fusion.1.refs_5_), channel_id=1, source_target_pairs={{1,24},{3,26},{4,29},{6,31}} | collective-permute-start | bytes 811016 | tf_op jit(solution)/shard_map/ppermute | solution.py:288
  20.0 15.2 %collective-permute-start.11 = (f32[2,264,128]{2,1,0:T(8,128)S(1)}, f32[2,264,128]{2,1,0:T(8,128)S(1)}, u32[]{:S(2)}, u32[]{:S(2)}) collective-permute-start(f32[2,264,128]{2,1,0:T(8,128)S(1)} %pad_maximum_fusion.refs_4_), channel_id=1, source_target_pairs={{1,16},{3,18},{4,21},{6,23},{9,24},{11,26},{12,29},{14,31}} | collective-permute-start | bytes 811016 | tf_op jit(solution)/shard_map/ppermute | solution.py:288
  21.3 15.2 %collective-permute-start.9 = (f32[2,264,128]{2,1,0:T(8,128)S(1)}, f32[2,264,128]{2,1,0:T(8,128)S(1)}, u32[]{:S(2)}, u32[]{:S(2)}) collective-permute-start(f32[2,264,128]{2,1,0:T(8,128)S(1)} %pad_maximum_fusion.refs_4_), channel_id=1, source_target_pairs={{0,16},{2,18},{5,21},{7,23},{8,24},{10,26},{13,29},{15,31}} | collective-permute-start | bytes 811016 | tf_op jit(solution)/shard_map/ppermute | solution.py:288
  22.7 18.5 %collective-permute-start.10 = (f32[2,264,128]{2,1,0:T(8,128)S(1)}, f32[2,264,128]{2,1,0:T(8,128)S(1)}, u32[]{:S(2)}, u32[]{:S(2)}) collective-permute-start(f32[2,264,128]{2,1,0:T(8,128)S(1)} %pad_maximum_fusion.1.refs_5_), channel_id=1, source_target_pairs={{0,16},{2,18},{5,21},{7,23},{8,24},{10,26},{13,29},{15,31}} | collective-permute-start | bytes 811016 | tf_op jit(solution)/shard_map/ppermute | solution.py:288
  29.0 13.5 %collective-permute-start.12 = (f32[2,264,128]{2,1,0:T(8,128)S(1)}, f32[2,264,128]{2,1,0:T(8,128)}, u32[]{:S(2)}, u32[]{:S(2)}) collective-permute-start(f32[2,264,128]{2,1,0:T(8,128)S(1)} %pad_maximum_fusion.1.refs_5_), channel_id=1, source_target_pairs={{1,16},{3,18},{4,21},{6,23},{9,24},{11,26},{12,29},{14,31}} | collective-permute-start | bytes 811016 | tf_op jit(solution)/shard_map/ppermute | solution.py:288
  30.2 13.5 %collective-permute-start.1 = (f32[2,264,128]{2,1,0:T(8,128)S(1)}, f32[2,264,128]{2,1,0:T(8,128)S(1)}, u32[]{:S(2)}, u32[]{:S(2)}) collective-permute-start(f32[2,264,128]{2,1,0:T(8,128)S(1)} %pad_maximum_fusion.refs_4_), channel_id=1, source_target_pairs={{0,8},{2,10},{5,13},{7,15},{8,16},{10,18},{13,21},{15,23},{16,24},... | collective-permute-start | bytes 811016 | tf_op jit(solution)/shard_map/ppermute | solution.py:288
  35.3 22.0 %collective-permute-start.5 = (f32[2,264,128]{2,1,0:T(8,128)S(1)}, f32[2,264,128]{2,1,0:T(8,128)}, u32[]{:S(2)}, u32[]{:S(2)}) collective-permute-start(f32[2,264,128]{2,1,0:T(8,128)S(1)} %pad_maximum_fusion.refs_4_), channel_id=1, source_target_pairs={{1,8},{3,10},{4,13},{6,15},{9,16},{11,18},{12,21},{14,23},{17,24},... | collective-permute-start | bytes 811016 | tf_op jit(solution)/shard_map/ppermute | solution.py:288
  36.6 20.7 %collective-permute-start.7 = (f32[2,264,128]{2,1,0:T(8,128)S(1)}, f32[2,264,128]{2,1,0:T(8,128)}, u32[]{:S(2)}, u32[]{:S(2)}) collective-permute-start(f32[2,264,128]{2,1,0:T(8,128)S(1)} %pad_maximum_fusion.refs_4_), channel_id=1, source_target_pairs={{1,0},{3,2},{4,5},{6,7},{9,8},{11,10},{12,13},{14,15},{17,16},{19,... | collective-permute-start | bytes 811016 | tf_op jit(solution)/shard_map/ppermute | solution.py:288
  41.2 16.1 %collective-permute-start.4 = (f32[2,264,128]{2,1,0:T(8,128)S(1)}, f32[2,264,128]{2,1,0:T(8,128)}, u32[]{:S(2)}, u32[]{:S(2)}) collective-permute-start(f32[2,264,128]{2,1,0:T(8,128)S(1)} %pad_maximum_fusion.1.refs_5_), channel_id=1, source_target_pairs={{0,8},{2,10},{5,13},{7,15},{8,16},{10,18},{13,21},{15,23},{16,24},... | collective-permute-start | bytes 811016 | tf_op jit(solution)/shard_map/ppermute | solution.py:288
  42.5 14.8 %collective-permute-start.6 = (f32[2,264,128]{2,1,0:T(8,128)S(1)}, f32[2,264,128]{2,1,0:T(8,128)}, u32[]{:S(2)}, u32[]{:S(2)}) collective-permute-start(f32[2,264,128]{2,1,0:T(8,128)S(1)} %pad_maximum_fusion.1.refs_5_), channel_id=1, source_target_pairs={{1,8},{3,10},{4,13},{6,15},{9,16},{11,18},{12,21},{14,23},{17,24},... | collective-permute-start | bytes 811016 | tf_op jit(solution)/shard_map/ppermute | solution.py:288
  43.8 13.5 %collective-permute-start.8 = (f32[2,264,128]{2,1,0:T(8,128)S(1)}, f32[2,264,128]{2,1,0:T(8,128)}, u32[]{:S(2)}, u32[]{:S(2)}) collective-permute-start(f32[2,264,128]{2,1,0:T(8,128)S(1)} %pad_maximum_fusion.1.refs_5_), channel_id=1, source_target_pairs={{1,0},{3,2},{4,5},{6,7},{9,8},{11,10},{12,13},{14,15},{17,16},{19,... | collective-permute-start | bytes 811016 | tf_op jit(solution)/shard_map/ppermute | solution.py:288
  69.1 5.9 %collective-permute-start.17 = (f32[256,128]{1,0:T(8,128)S(1)}, f32[256,128]{1,0:T(8,128)S(1)}, u32[]{:S(2)}, u32[]{:S(2)}) collective-permute-start(f32[256,128]{1,0:T(8,128)S(1)} %get-tuple-element.13), channel_id=1, source_target_pairs={{0,6},{2,4},{5,3},{7,1},{8,14},{10,12},{13,11},{15,9},{16,22},{18,... | collective-permute-start | bytes 393224 | tf_op jit(solution)/shard_map/ppermute | solution.py:332
  70.4 6.0 %collective-permute-start.18 = (f32[256,128]{1,0:T(8,128)S(1)}, f32[256,128]{1,0:T(8,128)S(1)}, u32[]{:S(2)}, u32[]{:S(2)}) collective-permute-start(f32[256,128]{1,0:T(8,128)S(1)} %get-tuple-element.16), channel_id=1, source_target_pairs={{0,4},{2,6},{5,1},{7,3},{8,12},{10,14},{13,9},{15,11},{16,20},{18,... | collective-permute-start | bytes 393224 | tf_op jit(solution)/shard_map/ppermute | solution.py:332
  71.7 6.9 %collective-permute-start.19 = (f32[256,128]{1,0:T(8,128)S(1)}, f32[256,128]{1,0:T(8,128)S(1)}, u32[]{:S(2)}, u32[]{:S(2)}) collective-permute-start(f32[256,128]{1,0:T(8,128)S(1)} %get-tuple-element.15), channel_id=1, source_target_pairs={{0,2},{2,0},{5,7},{7,5},{8,10},{10,8},{13,15},{15,13},{16,18},{18,... | collective-permute-start | bytes 393224 | tf_op jit(solution)/shard_map/ppermute | solution.py:332
